TPU v7x, 128 devices: a whole 4x4x4 slice. The times are simulated.
128 devices in a mesh: row: 8 (over z, x_lo), col: 16 (over x_hi, y, core).
Axes of the slice: x: 4 (x_hi: 2, x_lo: 2; x = x_hi * 2 + x_lo), y: 4, z: 4, core: 2. Of those that a mesh axis runs over, the one named last changes fastest.
Arguments:
- stream: float32 [16384, 256], P(('row', 'col')), may hold values from -130 to 130
- stream_tail: float32 [31, 256], replicated, may hold values from -130 to 130
- archive: float32 [65536, 256], P(('col', 'row')), may hold values from -60 to 60
- archive_tail: float32 [31, 256], replicated, may hold values from -60 to 60
Outputs:
- row_profile: float32 [16384], P(('row', 'col'))
- col_profile: float32 [65536], P(('col', 'row'))
All inputs are finite; a program needn't handle non-finite values.
Results may differ from a plain program's by a relative error of at most 0.0003.
Values sent between devices are 32-bit elements; how exact they have to be, the bound alone decides.
A program may use at most 128 MiB of HBM per device.

v0:
```python
import jax
import jax.numpy as jnp
from jax import lax
from jax.sharding import PartitionSpec as P

M = 32


def from_behind(block, axis, distance):
    devices = range(lax.axis_size(axis))
    route = [((i - distance) % len(devices), i) for i in devices]
    return lax.ppermute(block, axis, route)


def shifted(value, axis, steps):
    count = lax.axis_size(axis)
    leading, last = (max(0, -steps), min(count, count - steps))
    return lax.ppermute(value, axis, [(source, source + steps) for source in range(leading, last)])


def to_unit(frames):
    return frames / jnp.sqrt(jnp.sum(frames * frames, axis=1, keepdims=True) + 1e-06)


def window_sum(gram_block):
    summed = gram_block
    width = 1
    while width < M:
        height = summed.shape[0] - width
        breadth = summed.shape[1] - width
        summed = summed[0:height, 0:breadth] + summed[width:, width:]
        width = width * 2
    return summed


def profile_tile(stream_ext, archive_ext):
    row_count = stream_ext.shape[0] - (M - 1)
    col_count = archive_ext.shape[0] - (M - 1)
    block_rows = min(256, row_count)
    while block_rows * col_count < 2**20 and row_count % (block_rows * 2) == 0:
        block_rows = block_rows * 2
    steps_count = row_count // block_rows

    def advance(col_best, position):
        first_row = position * block_rows
        window_rows = lax.dynamic_slice_in_dim(stream_ext, first_row, block_rows + M - 1, 0)
        gram_block = lax.dot_general(
            window_rows,
            archive_ext,
            (((1,), (1,)), ((), ())),
            precision=lax.Precision.HIGHEST,
            preferred_element_type=jnp.float32,
        )
        scores = window_sum(gram_block) / M
        return (jnp.maximum(col_best, jnp.max(scores, axis=0)), jnp.max(scores, axis=1))

    start_best = jnp.full((col_count,), -2.0, jnp.float32)
    col_best, row_best = lax.scan(advance, start_best, jnp.arange(steps_count, dtype=jnp.int32))
    return (row_best.reshape(-1), col_best)


def on_device(stream, stream_tail, archive, archive_tail):
    stream_unit = to_unit(stream)
    archive_unit = to_unit(archive)
    stream_after = to_unit(stream_tail)
    archive_after = to_unit(archive_tail)
    last_row = lax.axis_index("row") == lax.axis_size("row") - 1
    last_col = lax.axis_index("col") == lax.axis_size("col") - 1
    stream_all = lax.all_gather(stream_unit, ("row", "col"), axis=0, tiled=True)
    stream_ext = jnp.concatenate([stream_all, stream_after], axis=0)
    head_rows = archive_unit[: M - 1]
    from_below = from_behind(head_rows, "row", -1)
    from_beside = shifted(from_below, "col", -1)
    following = jnp.where(last_row, jnp.where(last_col, archive_after, from_beside), from_below)
    archive_ext = jnp.concatenate([archive_unit, following], axis=0)
    row_best, col_profile = profile_tile(stream_ext, archive_ext)
    row_best = lax.pmax(row_best, ("row", "col"))
    own_len = stream.shape[0]
    flat_index = lax.axis_index("row") * lax.axis_size("col") + lax.axis_index("col")
    row_profile = lax.dynamic_slice_in_dim(row_best, flat_index * own_len, own_len)
    return (row_profile, col_profile)


def solution(mesh):
    return jax.shard_map(
        on_device,
        mesh=mesh,
        in_specs=(P(("row", "col"), None), P(), P(("col", "row"), None), P()),
        out_specs=(P(("row", "col")), P(("col", "row"))),
        check_vma=False,
    )
```

profile of v0, /device:TPU:1, one launch (start us, length us, event | category | flops | bytes accessed | tf_op | source)
XLA Modules:
  0.0 509.9 jit_solution(15961827501369002649)
XLA Ops:
  8.2 1.6 broadcast_divide_fusion.1
  12.4 5.6 %collective-permute-start = (f32[31,256]{1,0:T(8,128)S(1)}, f32[31,256]{1,0:T(8,128)S(1)}, u32[]{:S(2)}, u32[]{:S(2)}) collective-permute-start(f32[31,256]{1,0:T(8,128)S(1)} %slice.54), channel_id=1, source_target_pairs={{16,0},{32,16},{48,32},{64,48},{80,64},{96,80},{112,96},{0,112},{1... | collective-permute-start | bytes 95240 | tf_op jit(solution)/shard_map/ppermute | solution.py:12
  20.5 2.9 collective-permute-start.1
  23.4 2.8 collective-permute-done.1
  27.1 197.7 %all-gather.2.cloned.1.call-done = f32[16384,256]{1,0:T(8,128)} async-done(((f32[128,256]{1,0:T(8,128)}), f32[16384,256]{1,0:T(8,128)}) %all-gather.2.cloned.1.call-update) | async-done | bytes 16777232 | tf_op jit(solution)/shard_map/all_gather | solution.py:69
  224.8 14.4 %pad_maximum_fusion = f32[16415,256]{1,0:T(8,128)} fusion(f32[31,256]{1,0:T(8,128)S(1)} %broadcast_divide_fusion.2, f32[16384,256]{1,0:T(8,128)} %all-gather.2.cloned.1.call-done), kind=kLoop, calls=%fused_computation.12 | loop fusion | flops 4202240 | bytes 33617920 | tf_op jit(solution)/shard_map/concatenate | solution.py:70
  239.2 123.0 %while.13 = (s32[]{:T(128)}, f32[512]{0:T(512)S(1)}, f32[8,2048]{1,0:T(8,128)S(1)}, s32[8]{0:T(128)S(1)}, f32[16415,256]{1,0:T(8,128)}, /*index=5*/f32[543,256]{...) while((s32[]{:T(128)}, f32[512]{0:T(512)S(1)}, f32[8,2048]{1,0:T(8,128)S(1)}, ...), condition=%wide.region_7.8_spmd.clone, body=%wide.region_4.7_spmd.clone.sunk | while | flops 3476612096 | bytes 68995496 | solution.py:58
  240.5 6.3 %fusion.13 = f32[2079,543]{0,1:T(8,128)S(1)} fusion(f32[543,256]{1,0:T(8,128)S(1)} %get-tuple-element.138, f32[16415,256]{1,0:T(8,128)} %get-tuple-element.137, s32[]{:T(128)S(6)} %select_n.31), kind=kOutput, calls=%fused_computation.6.clone.1 | convolution fusion | flops 3467971584 | bytes 7201544 | tf_op jit(solution)/shard_map/while/body/eval_jaxpr/dot_general | solution.py:47
  246.8 1.7 slice_add_fusion.9
  248.5 1.7 slice_add_fusion.10
  255.9 6.3 %fusion.13 = f32[2079,543]{0,1:T(8,128)S(1)} fusion(f32[543,256]{1,0:T(8,128)S(1)} %get-tuple-element.138, f32[16415,256]{1,0:T(8,128)} %get-tuple-element.137, s32[]{:T(128)S(6)} %select_n.31), kind=kOutput, calls=%fused_computation.6.clone.1 | convolution fusion | flops 3467971584 | bytes 7201544 | tf_op jit(solution)/shard_map/while/body/eval_jaxpr/dot_general | solution.py:47
  262.2 1.7 slice_add_fusion.9
  263.9 1.7 slice_add_fusion.10
  271.3 6.3 %fusion.13 = f32[2079,543]{0,1:T(8,128)S(1)} fusion(f32[543,256]{1,0:T(8,128)S(1)} %get-tuple-element.138, f32[16415,256]{1,0:T(8,128)} %get-tuple-element.137, s32[]{:T(128)S(6)} %select_n.31), kind=kOutput, calls=%fused_computation.6.clone.1 | convolution fusion | flops 3467971584 | bytes 7201544 | tf_op jit(solution)/shard_map/while/body/eval_jaxpr/dot_general | solution.py:47
  277.6 1.7 slice_add_fusion.9
  279.3 1.7 slice_add_fusion.10
  286.6 6.3 %fusion.13 = f32[2079,543]{0,1:T(8,128)S(1)} fusion(f32[543,256]{1,0:T(8,128)S(1)} %get-tuple-element.138, f32[16415,256]{1,0:T(8,128)} %get-tuple-element.137, s32[]{:T(128)S(6)} %select_n.31), kind=kOutput, calls=%fused_computation.6.clone.1 | convolution fusion | flops 3467971584 | bytes 7201544 | tf_op jit(solution)/shard_map/while/body/eval_jaxpr/dot_general | solution.py:47
  293.0 1.7 slice_add_fusion.9
  294.6 1.7 slice_add_fusion.10
  302.0 6.3 %fusion.13 = f32[2079,543]{0,1:T(8,128)S(1)} fusion(f32[543,256]{1,0:T(8,128)S(1)} %get-tuple-element.138, f32[16415,256]{1,0:T(8,128)} %get-tuple-element.137, s32[]{:T(128)S(6)} %select_n.31), kind=kOutput, calls=%fused_computation.6.clone.1 | convolution fusion | flops 3467971584 | bytes 7201544 | tf_op jit(solution)/shard_map/while/body/eval_jaxpr/dot_general | solution.py:47
  308.4 1.7 slice_add_fusion.9
  310.0 1.7 slice_add_fusion.10
  317.4 6.3 %fusion.13 = f32[2079,543]{0,1:T(8,128)S(1)} fusion(f32[543,256]{1,0:T(8,128)S(1)} %get-tuple-element.138, f32[16415,256]{1,0:T(8,128)} %get-tuple-element.137, s32[]{:T(128)S(6)} %select_n.31), kind=kOutput, calls=%fused_computation.6.clone.1 | convolution fusion | flops 3467971584 | bytes 7201544 | tf_op jit(solution)/shard_map/while/body/eval_jaxpr/dot_general | solution.py:47
  323.7 1.7 slice_add_fusion.9
  325.4 1.7 slice_add_fusion.10
  332.8 6.3 %fusion.13 = f32[2079,543]{0,1:T(8,128)S(1)} fusion(f32[543,256]{1,0:T(8,128)S(1)} %get-tuple-element.138, f32[16415,256]{1,0:T(8,128)} %get-tuple-element.137, s32[]{:T(128)S(6)} %select_n.31), kind=kOutput, calls=%fused_computation.6.clone.1 | convolution fusion | flops 3467971584 | bytes 7201544 | tf_op jit(solution)/shard_map/while/body/eval_jaxpr/dot_general | solution.py:47
  339.1 1.7 slice_add_fusion.9
  340.8 1.7 slice_add_fusion.10
  348.2 6.3 %fusion.13 = f32[2079,543]{0,1:T(8,128)S(1)} fusion(f32[543,256]{1,0:T(8,128)S(1)} %get-tuple-element.138, f32[16415,256]{1,0:T(8,128)} %get-tuple-element.137, s32[]{:T(128)S(6)} %select_n.31), kind=kOutput, calls=%fused_computation.6.clone.1 | convolution fusion | flops 3467971584 | bytes 7201544 | tf_op jit(solution)/shard_map/while/body/eval_jaxpr/dot_general | solution.py:47
  354.5 1.7 slice_add_fusion.9
  356.2 1.7 slice_add_fusion.10
  363.0 138.8 %all-reduce.2.cloned.1.call-done = f32[16384]{0:T(1024)} async-done(((f32[16384]{0:T(1024)}), f32[16384]{0:T(1024)}) %all-reduce.2.cloned.1.call-update) | async-done | bytes 65552 | tf_op jit(solution)/shard_map/pmax | solution.py:77
  (73 shorter events, 48.9 us)
Async XLA Ops:
  7.2 217.6 %all-gather.2.cloned.1.call-start = ((), (), s32[]{:S(2)}) async-start(), calls=%async_computation | async-start | bytes 16908288 | tf_op jit(solution)/shard_map/all_gather | solution.py:69
  9.9 491.9 %all-reduce.2.cloned.1.call-start = ((), (), s32[]{:S(2)}) async-start(), calls=%async_computation.1 | async-start | bytes 131072 | tf_op jit(solution)/shard_map/pmax | solution.py:77
  12.4 8.2 %collective-permute-start = (f32[31,256]{1,0:T(8,128)S(1)}, f32[31,256]{1,0:T(8,128)S(1)}, u32[]{:S(2)}, u32[]{:S(2)}) collective-permute-start(f32[31,256]{1,0:T(8,128)S(1)} %slice.54), channel_id=1, source_target_pairs={{16,0},{32,16},{48,32},{64,48},{80,64},{96,80},{112,96},{0,112},{1... | collective-permute-start | bytes 95240 | tf_op jit(solution)/shard_map/ppermute | solution.py:12
  20.5 5.7 %collective-permute-start.1 = (f32[31,256]{1,0:T(8,128)S(1)}, f32[31,256]{1,0:T(8,128)S(1)}, u32[]{:S(2)}, u32[]{:S(2)}) collective-permute-start(f32[31,256]{1,0:T(8,128)S(1)} %collective-permute-done), channel_id=1, source_target_pairs={{1,0},{2,1},{3,2},{4,3},{5,4},{6,5},{7,6},{8,7},{9,8},{10,9},{11,1... | collective-permute-start | bytes 95240 | tf_op jit(solution)/shard_map/ppermute | solution.py:18
  362.3 140.8 %copy-start = (f32[512]{0:T(512)}, f32[512]{0:T(512)S(1)}, u32[]{:S(2)}) copy-start(f32[512]{0:T(512)S(1)} %get-tuple-element.34) | copy-start | bytes 6148
Sparse Core Ops, SparseCore 0:
  10.0 214.7 all-gather.1
  363.1 138.6 all-reduce.1
where the time goes:
time: 511 us; the launch traced here: 510 us
  waiting for transfers between devices  339 us (66%)
  other arithmetic  83.3 us (16%)
  matrix products  50.6 us (10%)
  between operations  14.2 us (3%)
  starting transfers between devices  8.51 us (2%)
  local copies, waits for them, and re-layouts  8.22 us (2%)
  loops' own time  5.71 us (1%)
    all_gather x1, waiting for transfers between devices, on_device(): stream_all = lax.all_gather(stream_unit, ('row', 'col'), axis=0, tiled=True)  198 us
    pmax x1, waiting for transfers between devices, on_device(): row_best = lax.pmax(row_best, ('row', 'col'))  139 us
    dot_general x8, matrix products, advance(): lax.dot_general(window_rows, archive_ext, (((1,), (1,)), ((), ())), preci...  50.6 us
    add x32, other arithmetic, window_sum(): summed = summed[0:height, 0:breadth] + summed[width:, width:]  49.6 us
    concatenate x1, other arithmetic, on_device(): stream_ext = jnp.concatenate([stream_all, stream_after], axis=0)  14.4 us
    reduce_max x8, other arithmetic, advance(): jnp.max(scores, axis=1)  10.6 us
  transfers between devices with their start and end apart: 4, of which 3 were waited for; matrix products, arithmetic and copies ran while one was open for 1% of the time, Pallas kernels for 0%

commit v1 on v0

v1 whole, which is shorter than its diff:
```python
import functools

import jax
import jax.numpy as jnp
from jax import lax
from jax.sharding import PartitionSpec as P
from jax.experimental import pallas as pl
from jax.experimental.pallas import tpu as pltpu
M=32; C=17; SEG=512; T=544; TV=512; PAD=32
NEG=-2.0*32
def prep_rhs(u_ref, b_ref):
    def one(c,_):
        xt = jnp.concatenate([u_ref.at[h][pl.ds(c, 128, stride=C), :].T for h in range(2)], axis=0)
        hi = xt.astype(jnp.bfloat16)
        lo = (xt - hi.astype(jnp.float32)).astype(jnp.bfloat16)
        n = pl.multiple_of(c*128,128)
        b_ref[0:256, pl.ds(n,128)] = hi
        b_ref[256:512, pl.ds(n,128)] = lo
        b_ref[512:768, pl.ds(n,128)] = hi
        return 0
    lax.fori_loop(0, C, one, 0)
def prep_lhs(v_ref, a_ref, t0, nt):
    def one(i,_):
        t = t0 + i*2
        x = jnp.concatenate([jnp.concatenate([v_ref.at[h][pl.ds(t+k, 8, stride=SEG), :] for k in range(2)], axis=0) for h in range(2)], axis=1)
        hi = x.astype(jnp.bfloat16)
        lo = (x - hi.astype(jnp.float32)).astype(jnp.bfloat16)
        r = pl.multiple_of(t*8, 16)
        a_ref[pl.ds(r,16), 0:256] = hi
        a_ref[pl.ds(r,16), 256:512] = hi
        a_ref[pl.ds(r,16), 512:768] = lo
        return 0
    lax.fori_loop(0, nt//2, one, 0, unroll=4)
DN = (((1,), (0,)), ((), ()))
def mm(a_ref, b_ref, g_ref, t0, nt, n, nw):
    r = pl.multiple_of(t0*8, 16)
    ro = pl.multiple_of((t0+PAD)*8, 16)
    g_ref[pl.ds(ro, nt*8), pl.ds(n, nw)] = lax.dot_general(a_ref[pl.ds(r, nt*8), :], b_ref[:, pl.ds(n, nw)], DN, preferred_element_type=jnp.float32)
def vstep(g_ref, t, E, R, tm_ref, out):
    row = pl.multiple_of((t+PAD)*8, 8)
    old = pl.multiple_of(t*8, 8)
    N = []
    for c in range(C):
        g = g_ref[pl.ds(row,8), c*128:(c+1)*128]
        tile, sh = (c+2, 2) if c+2 < C else (c+2-C, 1)
        go = pltpu.roll(g_ref[pl.ds(old,8), tile*128:(tile+1)*128], sh, 1)
        ep = E[c-1] if c else pltpu.roll(E[C-1], 1, 1)
        N.append(ep + (g - go))
    if out:
        R = [jnp.maximum(r, e) for r, e in zip(R, N)]
        mx = functools.reduce(jnp.maximum, N[5:14])
        mb = functools.reduce(jnp.maximum, N[0:5])
        mc = functools.reduce(jnp.maximum, N[14:17])
        lane = lax.broadcasted_iota(jnp.int32, (8,128), 1)
        neg = jnp.float32(NEG)
        mid = (lane >= 2) & (lane <= 121)
        m = jnp.where(mid, mx, neg)
        m = jnp.maximum(m, jnp.where((lane>=2)&(lane<=122), mb, neg))
        m = jnp.maximum(m, jnp.where((lane>=1)&(lane<=121), mc, neg))
        tm_ref[pl.ds(pl.multiple_of((t-31)*8,8), 8), :] = m
    return N, R
def compute(a_ref, b_ref, g_ref, tm_ref, NT=2):
    zero = jnp.zeros((8,128), jnp.float32)
    g_ref[0:PAD*8, :] = jnp.zeros((PAD*8, C*128), jnp.float32)
    lax.fori_loop(0, 8, lambda j,_: (mm(a_ref,b_ref,g_ref,0,96,pl.multiple_of(j*256,256),256),0)[1], 0)
    mm(a_ref,b_ref,g_ref,0,96,2048,128)
    E=[zero]*C; R=[jnp.full((8,128),NEG,jnp.float32)]*C
    def warm(t, c):
        n,_ = vstep(g_ref, t, list(c), R, tm_ref, False)
        return tuple(n)
    E = lax.fori_loop(0, 31, warm, tuple(E))
    def blk(b, carry):
        t0 = 96+64*b
        def inner(j, carry):
            E,R = list(carry[0]), list(carry[1])
            mm(a_ref,b_ref,g_ref,t0,64,pl.multiple_of(j*256*NT,256),256*NT)
            for k in range(8*NT):
                E,R = vstep(g_ref, 31+64*b + j*8*NT + k, E, R, tm_ref, True)
            return tuple(E), tuple(R)
        carry = lax.fori_loop(0, 8//NT, inner, carry)
        mm(a_ref,b_ref,g_ref,t0,64,2048,128)
        return carry
    carry = lax.fori_loop(0, 7, blk, (tuple(E),tuple(R)))
    def fin(j, carry):
        E,R = list(carry[0]), list(carry[1])
        for k in range(8):
            E,R = vstep(g_ref, 31+448 + j*8 + k, E, R, tm_ref, True)
        return tuple(E), tuple(R)
    E,R = lax.fori_loop(0, 8, fin, carry)
    return R
def finish(tm_ref, R, col_ref, row_ref):
    def one(s,_):
        rows=[]
        for tb in range(4):
            x = tm_ref[pl.ds(s + tb*1024, 128, stride=8), :]
            rows.append(jnp.max(x.T, axis=0, keepdims=True))
        col_ref[pl.ds(s,1),:] = jnp.concatenate(rows, axis=1)*(1.0/M)
        return 0
    lax.fori_loop(0, 8, one, 0)
    for c in range(C):
        row_ref[c:c+1,:] = jnp.max(R[c], axis=0, keepdims=True)*(1.0/M)
    row_ref[C:24,:] = jnp.full((7,128), -2.0, jnp.float32)

def kern(v_ref, u_ref, col_ref, row_ref, a, b, g, tm):
    prep_rhs(u_ref, b)
    prep_lhs(v_ref, a, 0, T)
    R = compute(a, b, g, tm, 4)
    finish(tm, R, col_ref, row_ref)

def call(v, u):
    vm = pl.BlockSpec(memory_space=pltpu.VMEM)
    return pl.pallas_call(
        kern,
        out_shape=(jax.ShapeDtypeStruct((8, 512), jnp.float32), jax.ShapeDtypeStruct((24, 128), jnp.float32)),
        in_specs=[vm, vm], out_specs=(vm, vm),
        scratch_shapes=[
            pltpu.VMEM((T*8, 768), jnp.bfloat16),
            pltpu.VMEM((768, C*128), jnp.bfloat16),
            pltpu.VMEM(((T+PAD)*8, C*128), jnp.float32),
            pltpu.VMEM((TV*8, 128), jnp.float32),
        ],
        compiler_params=pltpu.CompilerParams(vmem_limit_bytes=67043328),
        name="profile_tile")(v, u)

def to_unit(frames):
    return frames / jnp.sqrt(jnp.sum(frames * frames, axis=1, keepdims=True) + 1e-06)

def planes(x, rows):
    x = jnp.pad(x, ((0, rows - x.shape[0]), (0, 0)))
    return jnp.stack([x[:, :128], x[:, 128:]])

def on_device(stream, stream_tail, archive, archive_tail):
    r, c = lax.axis_index("row"), lax.axis_index("col")
    nr, nc = lax.axis_size("row"), lax.axis_size("col")
    su, au = to_unit(stream), to_unit(archive)
    st, at = to_unit(stream_tail), to_unit(archive_tail)
    s_blk = lax.all_gather(su, "col", axis=0, tiled=True)
    a_blk = lax.all_gather(au, "row", axis=0, tiled=True)
    s_head = lax.ppermute(s_blk[:31], "row", [(i, i - 1) for i in range(1, nr)])
    a_head = lax.ppermute(a_blk[:31], "col", [(i, i - 1) for i in range(1, nc)])
    s_head = jnp.where(r == nr - 1, st, s_head)
    a_head = jnp.where(c == nc - 1, at, a_head)
    u = planes(jnp.concatenate([s_blk, s_head]), C*128)
    v = planes(jnp.concatenate([a_blk, a_head]), 4128)
    col, row = call(v, u)
    row = row[:C].T.reshape(-1)[31:31 + 2048].reshape(16, 128)
    row = jnp.max(lax.all_to_all(row, "col", 0, 0, tiled=True), axis=0)
    col = jnp.max(lax.all_to_all(col, "row", 0, 0, tiled=True), axis=0)
    return row, col

def solution(mesh):
    return jax.shard_map(
        on_device, mesh=mesh,
        in_specs=(P(("row", "col"), None), P(), P(("col", "row"), None), P()),
        out_specs=(P(("row", "col")), P(("col", "row"))),
        check_vma=False)
```

time: 511 us -> 244 us (0.48)
  waiting for transfers between devices: 339 us -> 146 us
  other arithmetic: 83.3 us -> 13.1 us
  matrix products: 50.6 us -> 0 us
  Pallas kernels: 0 us -> 48.7 us
  starting transfers between devices: 8.51 us -> 15.2 us
  loops' own time: 5.71 us -> 0 us
    pmax x1 -> x0, waiting for transfers between devices: 139 us -> none  [on_device(): row_best = lax.pmax(row_best, ('row', 'col'))]
    all_gather x1 -> x2, waiting for transfers between devices: 198 us -> 131 us  [the longest x1 83.2 us: on_device(): a_blk = lax.all_gather(au, 'row', axis=0, tiled=True)]
    dot_general x8 -> x0, matrix products: 50.6 us -> none  [advance(): lax.dot_general(window_rows, archive_ext, (((1,), (1,)), ((), ())), preci...]
    add x32 -> x0, other arithmetic: 49.6 us -> none  [window_sum(): summed = summed[0:height, 0:breadth] + summed[width:, width:]]
    pallas_call x0 -> x1, Pallas kernels: none -> 48.7 us  [call(): pl.pallas_call(kern, out_shape=(jax.ShapeDtypeStruct((8, 512), jnp.float3...]
    concatenate x2, other arithmetic: 14.5 us -> 2.01 us  [the longest x1 1.74 us: on_device(): u = planes(jnp.concatenate([s_blk, s_head]), C * 128)]
    all_to_all x0 -> x2, starting transfers between devices: none -> 10.8 us  [the longest x1 7 us: on_device(): row = jnp.max(lax.all_to_all(row, 'col', 0, 0, tiled=True), axis=0)]
    all_to_all x0 -> x2, waiting for transfers between devices: none -> 10.2 us  [the longest x1 5.68 us: on_device(): row = jnp.max(lax.all_to_all(row, 'col', 0, 0, tiled=True), axis=0)]
  transfers between devices with their start and end apart: 4 -> 6, of which waited for: 3 -> 6; matrix products, arithmetic and copies ran while one was open for 1% -> 4% of each run, Pallas kernels for 0% -> 0%
where the time goes in v1:
time: 244 us; the launch traced here: 242 us
  waiting for transfers between devices  146 us (60%)
  Pallas kernels  48.7 us (20%)
  starting transfers between devices  15.2 us (6%)
  between operations  14.2 us (6%)
  other arithmetic  13.1 us (5%)
  local copies, waits for them, and re-layouts  5.21 us (2%)
    all_gather x1, waiting for transfers between devices, on_device(): a_blk = lax.all_gather(au, 'row', axis=0, tiled=True)  83.2 us
    pallas_call x1, Pallas kernels, call(): pl.pallas_call(kern, out_shape=(jax.ShapeDtypeStruct((8, 512), jnp.float3...  48.7 us
    all_gather x1, waiting for transfers between devices, on_device(): s_blk = lax.all_gather(su, 'col', axis=0, tiled=True)  48 us
    all_to_all x1, starting transfers between devices, on_device(): row = jnp.max(lax.all_to_all(row, 'col', 0, 0, tiled=True), axis=0)  7 us
    all_to_all x1, waiting for transfers between devices, on_device(): row = jnp.max(lax.all_to_all(row, 'col', 0, 0, tiled=True), axis=0)  5.68 us
  transfers between devices with their start and end apart: 6, of which 6 were waited for; matrix products, arithmetic and copies ran while one was open for 4% of the time, Pallas kernels for 0%

profile of v1, /device:TPU:1, one launch (start us, length us, event | category | flops | bytes accessed | tf_op | source)
XLA Modules:
  0.0 242.4 jit_solution(7038458538331201590)
XLA Ops:
  7.2 1.0 multiply_reduce_fusion.1
  8.3 1.7 broadcast_divide_fusion.1
  10.0 1.2 multiply_reduce_fusion
  11.2 2.0 broadcast_divide_fusion
  13.3 0.1 multiply_reduce_fusion.2
  13.5 48.0 %all-gather.5.cloned.1.call-done = f32[2048,256]{1,0:T(8,128)} async-done(((f32[128,256]{1,0:T(8,128)}), f32[2048,256]{1,0:T(8,128)}) %all-gather.5.cloned.1.call-update) | async-done | bytes 2097168 | tf_op jit(solution)/shard_map/all_gather | solution.py:137
  61.5 0.8 slice.35
  62.3 1.3 collective-permute-start.1
  63.6 3.3 %collective-permute-done.1 = f32[31,256]{1,0:T(8,128)S(1)} collective-permute-done((f32[31,256]{1,0:T(8,128)S(1)}, f32[31,256]{1,0:T(8,128)S(1)}, u32[]{:S(2)}, u32[]{:S(2)}) %collective-permute-start.1) | collective-permute-done | bytes 31776 | tf_op jit(solution)/shard_map/ppermute | solution.py:139
  67.0 1.7 select_maximum_fusion.1
  68.7 0.1 slice_bitcast_fusion.3
  68.9 83.2 %all-gather.3.cloned.1.call-done = f32[4096,256]{1,0:T(8,128)} async-done(((f32[512,256]{1,0:T(8,128)}), f32[4096,256]{1,0:T(8,128)}) %all-gather.3.cloned.1.call-update) | async-done | bytes 4194320 | tf_op jit(solution)/shard_map/all_gather | solution.py:138
  152.1 0.8 slice.32
  152.9 3.1 %collective-permute-start = (f32[31,256]{1,0:T(8,128)S(1)}, f32[31,256]{1,0:T(8,128)S(1)}, u32[]{:S(2)}, u32[]{:S(2)}) collective-permute-start(f32[31,256]{1,0:T(8,128)S(1)} %slice.32), channel_id=1, source_target_pairs={{1,0},{2,1},{3,2},{4,3},{5,4},{6,5},{7,6},{8,7},{9,8},{10,9},{11,1... | collective-permute-start | bytes 95240 | tf_op jit(solution)/shard_map/ppermute | solution.py:140
  156.0 1.5 pad_maximum_fusion.1.u_ref
  157.5 1.1 collective-permute-done
  158.7 0.2 copy-done
  158.9 0.3 select_maximum_fusion
  159.2 0.3 slice_bitcast_fusion.1
  159.5 2.2 pad_maximum_fusion.v_ref
  161.7 48.7 %profile_tile.1 = (f32[8,512]{1,0:T(8,128)}, f32[24,128]{1,0:T(8,128)}) custom-call(f32[2,4128,128]{2,1,0:T(8,128)} %pad_maximum_fusion.v_ref, f32[2,2176,128]{2,1,0:T(8,128)} %pad_maximum_fusion.1.u_ref), custom_call_target="tpu_custom_call" | custom-call | tf_op jit(solution)/shard_map/profile_tile/pallas_call | solution.py:112
  210.4 0.7 slice_bitcast_fusion.4
  211.1 0.1 copy.11
  211.2 0.2 reshape.37
  211.4 0.7 slice.38
  212.1 7.0 %all-to-all-start = ((f32[16,1,128]{2,1,0:T(1,128)}), f32[16,1,128]{2,1,0:T(1,128)S(1)}, u32[]{:S(2)}, u32[]{:S(2)}) async-start(f32[16,1,128]{2,1,0:T(1,128)} %bitcast.5), calls=%async_computation | async-start | bytes 16384 | tf_op jit(solution)/shard_map/all_to_all | solution.py:147
  219.1 1.3 copy.13
  220.4 5.7 %all-to-all-done = f32[16,1,128]{2,1,0:T(1,128)S(1)} async-done(((f32[16,1,128]{2,1,0:T(1,128)}), f32[16,1,128]{2,1,0:T(1,128)S(1)}, u32[]{:S(2)}, u32[]{:S(2)}) %all-to-all-start) | async-done | bytes 8224 | tf_op jit(solution)/shard_map/all_to_all | solution.py:147
  226.1 3.8 %all-to-all-start.1 = ((f32[8,1,512]{2,1,0:T(1,128)}), f32[8,1,512]{2,1,0:T(1,128)S(1)}, u32[]{:S(2)}, u32[]{:S(2)}) async-start(f32[8,1,512]{2,1,0:T(1,128)} %copy.13), calls=%async_computation.1 | async-start | bytes 32768 | tf_op jit(solution)/shard_map/all_to_all | solution.py:148
  229.9 0.5 reduce_max.18
  230.5 4.5 %all-to-all-done.1 = f32[8,1,512]{2,1,0:T(1,128)S(1)} async-done(((f32[8,1,512]{2,1,0:T(1,128)}), f32[8,1,512]{2,1,0:T(1,128)S(1)}, u32[]{:S(2)}, u32[]{:S(2)}) %all-to-all-start.1) | async-done | bytes 16416 | tf_op jit(solution)/shard_map/all_to_all | solution.py:148
  235.0 0.6 reduce_max.19
  (16 shorter events, 0.4 us)
Async XLA Ops:
  7.2 6.0 %copy-start.2 = (f32[31,256]{1,0:T(8,128)S(1)}, f32[31,256]{1,0:T(8,128)}, u32[]{:S(2)}) copy-start(f32[31,256]{1,0:T(8,128)} %param.7) | copy-start | bytes 95236
  7.2 6.2 %copy-start.1 = (f32[31,256]{1,0:T(8,128)S(1)}, f32[31,256]{1,0:T(8,128)}, u32[]{:S(2)}) copy-start(f32[31,256]{1,0:T(8,128)} %param.5) | copy-start | bytes 95236
  7.2 54.3 %all-gather.5.cloned.1.call-start = ((), (), s32[]{:S(2)}) async-start(), calls=%async_computation.3 | async-start | bytes 2228224 | tf_op jit(solution)/shard_map/all_gather | solution.py:137
  9.9 142.2 %all-gather.3.cloned.1.call-start = ((), (), s32[]{:S(2)}) async-start(), calls=%async_computation.2 | async-start | bytes 4718592 | tf_op jit(solution)/shard_map/all_gather | solution.py:138
  62.3 4.6 %collective-permute-start.1 = (f32[31,256]{1,0:T(8,128)S(1)}, f32[31,256]{1,0:T(8,128)S(1)}, u32[]{:S(2)}, u32[]{:S(2)}) collective-permute-start(f32[31,256]{1,0:T(8,128)S(1)} %slice.35), channel_id=1, source_target_pairs={{16,0},{32,16},{48,32},{64,48},{80,64},{96,80},{112,96},{17,1},{33... | collective-permute-start | bytes 95240 | tf_op jit(solution)/shard_map/ppermute | solution.py:139
  152.9 5.8 %collective-permute-start = (f32[31,256]{1,0:T(8,128)S(1)}, f32[31,256]{1,0:T(8,128)S(1)}, u32[]{:S(2)}, u32[]{:S(2)}) collective-permute-start(f32[31,256]{1,0:T(8,128)S(1)} %slice.32), channel_id=1, source_target_pairs={{1,0},{2,1},{3,2},{4,3},{5,4},{6,5},{7,6},{8,7},{9,8},{10,9},{11,1... | collective-permute-start | bytes 95240 | tf_op jit(solution)/shard_map/ppermute | solution.py:140
  155.9 3.0 %copy-start = (f32[4096,256]{1,0:T(8,128)S(1)}, f32[4096,256]{1,0:T(8,128)}, u32[]{:S(2)}) copy-start(f32[4096,256]{1,0:T(8,128)} %all-gather.3.cloned.1.call-done) | copy-start | bytes 12582916
  212.1 14.0 %all-to-all-start = ((f32[16,1,128]{2,1,0:T(1,128)}), f32[16,1,128]{2,1,0:T(1,128)S(1)}, u32[]{:S(2)}, u32[]{:S(2)}) async-start(f32[16,1,128]{2,1,0:T(1,128)} %bitcast.5), calls=%async_computation | async-start | bytes 16384 | tf_op jit(solution)/shard_map/all_to_all | solution.py:147
  226.1 8.9 %all-to-all-start.1 = ((f32[8,1,512]{2,1,0:T(1,128)}), f32[8,1,512]{2,1,0:T(1,128)S(1)}, u32[]{:S(2)}, u32[]{:S(2)}) async-start(f32[8,1,512]{2,1,0:T(1,128)} %copy.13), calls=%async_computation.1 | async-start | bytes 32768 | tf_op jit(solution)/shard_map/all_to_all | solution.py:148
Sparse Core Ops, SparseCore 0:
  10.5 50.9 all-gather.4
  63.1 88.9 all-gather.2

commit v2 on v1

--- a/solution.py
+++ b/solution.py
@@ -89,17 +89,23 @@
     E,R = lax.fori_loop(0, 8, fin, carry)
     return R
 def finish(tm_ref, R, col_ref, row_ref):
-    def one(s,_):
-        rows=[]
+    def one(s, _):
         for tb in range(4):
             x = tm_ref[pl.ds(s + tb*1024, 128, stride=8), :]
-            rows.append(jnp.max(x.T, axis=0, keepdims=True))
-        col_ref[pl.ds(s,1),:] = jnp.concatenate(rows, axis=1)*(1.0/M)
+            col_ref[s, 0:1, tb*128:(tb+1)*128] = jnp.max(x.T, axis=0, keepdims=True)*(1.0/M)
         return 0
     lax.fori_loop(0, 8, one, 0)
-    for c in range(C):
-        row_ref[c:c+1,:] = jnp.max(R[c], axis=0, keepdims=True)*(1.0/M)
-    row_ref[C:24,:] = jnp.full((7,128), -2.0, jnp.float32)
+    rows = jnp.concatenate([jnp.max(r, axis=0, keepdims=True) for r in R] + [jnp.full((7, 128), NEG, jnp.float32)], axis=0)*(1.0/M)
+    for j in range(4):
+        q = lax.broadcasted_iota(jnp.int32, (128, 512), 1) + (31 + 512*j)
+        pick = (lax.broadcasted_iota(jnp.int32, (128, 512), 0) == ((q*3856) >> 16)).astype(jnp.float32)
+        x = lax.dot_general(rows, pick, DN, precision=lax.Precision.HIGHEST, preferred_element_type=jnp.float32)
+        q = lax.broadcasted_iota(jnp.int32, (24, 512), 1) + (31 + 512*j)
+        lane = (q*3856) >> 16
+        x = jnp.where(lax.broadcasted_iota(jnp.int32, (24, 512), 0) == q - lane*C, x, 0.0)
+        x = jnp.sum(x, axis=0, keepdims=True)
+        for m in range(4):
+            row_ref[4*j + m, 0:1, :] = x[:, 128*m:128*(m+1)]
 
 def kern(v_ref, u_ref, col_ref, row_ref, a, b, g, tm):
     prep_rhs(u_ref, b)
@@ -107,12 +113,15 @@
     R = compute(a, b, g, tm, 4)
     finish(tm, R, col_ref, row_ref)
 
+VM = pl.BlockSpec(memory_space=pltpu.VMEM)
+ANY = pl.BlockSpec(memory_space=pl.ANY)
+F32 = jnp.float32
+
 def call(v, u):
-    vm = pl.BlockSpec(memory_space=pltpu.VMEM)
     return pl.pallas_call(
         kern,
-        out_shape=(jax.ShapeDtypeStruct((8, 512), jnp.float32), jax.ShapeDtypeStruct((24, 128), jnp.float32)),
-        in_specs=[vm, vm], out_specs=(vm, vm),
+        out_shape=(jax.ShapeDtypeStruct((8, 1, 512), F32), jax.ShapeDtypeStruct((16, 1, 128), F32)),
+        in_specs=[VM, VM], out_specs=(VM, VM),
         scratch_shapes=[
             pltpu.VMEM((T*8, 768), jnp.bfloat16),
             pltpu.VMEM((768, C*128), jnp.bfloat16),
@@ -122,31 +131,189 @@
         compiler_params=pltpu.CompilerParams(vmem_limit_bytes=67043328),
         name="profile_tile")(v, u)
 
-def to_unit(frames):
-    return frames / jnp.sqrt(jnp.sum(frames * frames, axis=1, keepdims=True) + 1e-06)
-
-def planes(x, rows):
-    x = jnp.pad(x, ((0, rows - x.shape[0]), (0, 0)))
-    return jnp.stack([x[:, :128], x[:, 128:]])
+MESH = pl.DeviceIdType.MESH
+
+def place():
+    row, col = lax.axis_index("row"), lax.axis_index("col")
+    z, x_lo = row // 2, row % 2
+    x_hi, y, k = col // 8, (col // 2) % 4, col % 2
+    return row, col, x_hi, x_lo, y, z, k
+
+def dev(x, y, z, k):
+    return (z*2 + x % 2, (x // 2)*8 + y*2 + k)
+
+def unit(x):
+    return x / jnp.sqrt(jnp.sum(x*x, axis=1, keepdims=True) + 1e-06)
+
+def put_planes(dst, x):
+    dst[0] = x[:, :128]
+    dst[1] = x[:, 128:]
+
+NQ = 4
+CH = 512 // NQ
+
+def gather_kern(s_ref, st_ref, a_ref, at_ref, v_ref, u_ref, su, av, tails, zeros, send, got_v, got_u, misc):
+    row, col, x_hi, x_lo, y, z, k = place()
+    x = x_hi*2 + x_lo
+    waits = []
+    count = [0]
+
+    def remote(src, dst, sem, to, when=None):
+        c = pltpu.make_async_remote_copy(src_ref=src, dst_ref=dst, send_sem=send.at[count[0]], recv_sem=sem, device_id=to, device_id_type=MESH)
+        count[0] += 1
+        waits.append((c, when))
+        if when is None:
+            c.start()
+        else:
+            pl.when(when)(c.start)
+
+    def arrived(ref, sem):
+        pltpu.make_async_copy(ref, ref, sem).wait()
+
+    def vs(b, q):
+        return v_ref.at[:, pl.ds(pl.multiple_of(b*512 + q*CH, CH), CH), :]
+
+    def us(b):
+        return u_ref.at[:, pl.ds(pl.multiple_of(b*128, 128), 128), :]
+
+    put_planes(av, unit(a_ref[...]))
+    put_planes(su, unit(s_ref[...]))
+    zero = jnp.zeros((1, 256), F32)
+    put_planes(tails.at[0], jnp.concatenate([unit(st_ref[...]), zero], axis=0))
+    put_planes(tails.at[1], jnp.concatenate([unit(at_ref[...]), zero], axis=0))
+    zeros[...] = jnp.zeros(zeros.shape, F32)
+    home = x_lo == k
+    away = x_lo != k
+    for q in range(NQ):
+        src = av.at[:, pl.ds(q*CH, CH), :]
+        local = pltpu.make_async_copy(src, vs(row, q), got_v.at[row, q])
+        pl.when(home)(local.start)
+        remote(src, vs(row, q), got_v.at[row, q], dev(x_hi*2 + k, y, z, 1 - k), away)
+    own = pltpu.make_async_copy(su, us(col), got_u.at[col])
+    pl.when(home)(own.start)
+    remote(su, us(col), got_u.at[col], dev(x, y, z, 1 - k), away)
+    for p in (1, 3, 2):
+        remote(su, us(col), got_u.at[col], dev((x + p*k) % 4, (y + p*(1 - k)) % 4, z, x_lo))
+    pad = pltpu.make_async_copy(zeros, u_ref.at[:, pl.ds(2080, 96), :], misc.at[0])
+    pad.start()
+    bo = z*2 + k
+    up, dn, far = (z + 1) % 4, (z + 3) % 4, (z + 2) % 4
+    for q in range(NQ):
+        arrived(vs(bo, q), got_v.at[bo, q])
+        remote(vs(bo, q), vs(bo, q), got_v.at[bo, q], dev(x, y, up, k))
+        remote(vs(bo, q), vs(bo, q), got_v.at[bo, q], dev(x, y, dn, k))
+        remote(vs(bo, q), vs(bo, q), got_v.at[bo, q], dev(x, y, z, 1 - k))
+    for xs in range(2):
+        b = xs*8 + y*2 + 1
+        arrived(us(b), got_u.at[b])
+        for p in (1, 3, 2):
+            remote(us(b), us(b), got_u.at[b], dev(x, (y + p) % 4, z, k))
+    for yy in range(4):
+        b = x_hi*8 + yy*2
+        pl.when(home)(lambda b=b: arrived(us(b), got_u.at[b]))
+        for p in (1, 3, 2):
+            remote(us(b), us(b), got_u.at[b], dev((x + p) % 4, y, z, k), home)
+    bu, bd, bf = up*2 + k, dn*2 + k, far*2 + k
+    for q in range(NQ):
+        arrived(vs(bd, q), got_v.at[bd, q])
+        if q % 2 == 0:
+            remote(vs(bd, q), vs(bd, q), got_v.at[bd, q], dev(x, y, up, k))
+        remote(vs(bd, q), vs(bd, q), got_v.at[bd, q], dev(x, y, z, 1 - k))
+        arrived(vs(bu, q), got_v.at[bu, q])
+        if q % 2 == 1:
+            remote(vs(bu, q), vs(bu, q), got_v.at[bu, q], dev(x, y, dn, k))
+        remote(vs(bu, q), vs(bu, q), got_v.at[bu, q], dev(x, y, z, 1 - k))
+    for q in range(NQ):
+        arrived(vs(bf, q), got_v.at[bf, q])
+        remote(vs(bf, q), vs(bf, q), got_v.at[bf, q], dev(x, y, z, 1 - k))
+    for zz in range(4):
+        for q in range(NQ):
+            b = zz*2 + 1 - k
+            arrived(vs(b, q), got_v.at[b, q])
+    for xs in range(2):
+        for yy in range(4):
+            b = xs*8 + yy*2 + 1
+            pl.when(yy != y)(lambda b=b: arrived(us(b), got_u.at[b]))
+            b = xs*8 + yy*2
+            pl.when(jnp.logical_or(away, xs != x_hi))(lambda b=b: arrived(us(b), got_u.at[b]))
+    cb = (x_hi*4 + y)*2 + x_lo
+    pc = (cb + 15) % 16
+    rb = z*2 + k
+    pr = (rb + 7) % 8
+    remote(v_ref.at[:, pl.ds(0, 32), :], v_ref.at[:, pl.ds(4096, 32), :], misc.at[1], dev((pc // 8)*2 + pc % 2, (pc // 2) % 4, z, k), cb != 0)
+    remote(u_ref.at[:, pl.ds(0, 32), :], u_ref.at[:, pl.ds(2048, 32), :], misc.at[2], dev(x, y, pr // 2, pr % 2), rb != 0)
+    tv = pltpu.make_async_copy(tails.at[1], v_ref.at[:, pl.ds(4096, 32), :], misc.at[1])
+    tu = pltpu.make_async_copy(tails.at[0], u_ref.at[:, pl.ds(2048, 32), :], misc.at[2])
+    pl.when(cb == 15)(tv.start)
+    pl.when(rb == 7)(tu.start)
+    tv.wait()
+    tu.wait()
+    pad.wait()
+    for c, when in waits:
+        if when is None:
+            c.wait_send()
+        else:
+            pl.when(when)(c.wait_send)
+
+def gather(s, st, a, at):
+    return pl.pallas_call(
+        gather_kern,
+        out_shape=(jax.ShapeDtypeStruct((2, 4128, 128), F32), jax.ShapeDtypeStruct((2, 2176, 128), F32)),
+        in_specs=[VM]*4, out_specs=(ANY, ANY),
+        scratch_shapes=[
+            pltpu.VMEM((2, 128, 128), F32), pltpu.VMEM((2, 512, 128), F32),
+            pltpu.VMEM((2, 2, 32, 128), F32), pltpu.VMEM((2, 96, 128), F32),
+            pltpu.SemaphoreType.DMA((72,)), pltpu.SemaphoreType.DMA((8, NQ)), pltpu.SemaphoreType.DMA((16,)), pltpu.SemaphoreType.DMA((3,)),
+        ],
+        compiler_params=pltpu.CompilerParams(has_side_effects=True),
+        name="gather_frames")(s, st, a, at)
+
+def exchange_kern(col_ref, row_ref, colp_ref, rowp_ref, cbuf, rbuf, csend, rsend, cgot, rgot):
+    row, col, x_hi, x_lo, y, z, k = place()
+    rb = z*2 + k
+    me_r = x_hi*8 + y*2 + x_lo
+    home = x_lo == k
+    cp = []
+    for s in range(8):
+        other = jnp.logical_or(row != s, x_lo != k)
+        c = pltpu.make_async_remote_copy(src_ref=col_ref.at[s], dst_ref=cbuf.at[rb], send_sem=csend.at[s], recv_sem=cgot.at[rb], device_id=(s, me_r), device_id_type=MESH)
+        pl.when(other)(c.start)
+        cp.append((c, other))
+    for j in range(16):
+        other = jnp.logical_or(col != j, x_lo != k)
+        c = pltpu.make_async_remote_copy(src_ref=row_ref.at[j], dst_ref=rbuf.at[me_r], send_sem=rsend.at[j], recv_sem=rgot.at[me_r], device_id=(rb, j), device_id_type=MESH)
+        pl.when(other)(c.start)
+        cp.append((c, other))
+    lc = pltpu.make_async_copy(col_ref.at[row], cbuf.at[rb], cgot.at[rb])
+    lr = pltpu.make_async_copy(row_ref.at[col], rbuf.at[me_r], rgot.at[me_r])
+    pl.when(home)(lc.start)
+    pl.when(home)(lr.start)
+    for s in range(8):
+        pltpu.make_async_copy(cbuf.at[s], cbuf.at[s], cgot.at[s]).wait()
+    for j in range(16):
+        pltpu.make_async_copy(rbuf.at[j], rbuf.at[j], rgot.at[j]).wait()
+    colp_ref[...] = functools.reduce(jnp.maximum, [cbuf[s] for s in range(8)])
+    rowp_ref[...] = functools.reduce(jnp.maximum, [rbuf[j] for j in range(16)])
+    for c, other in cp:
+        pl.when(other)(c.wait_send)
+
+def exchange(col, row):
+    return pl.pallas_call(
+        exchange_kern,
+        out_shape=(jax.ShapeDtypeStruct((1, 512), F32), jax.ShapeDtypeStruct((1, 128), F32)),
+        in_specs=[VM, VM], out_specs=(VM, VM),
+        scratch_shapes=[
+            pltpu.VMEM((8, 1, 512), F32), pltpu.VMEM((16, 1, 128), F32),
+            pltpu.SemaphoreType.DMA((8,)), pltpu.SemaphoreType.DMA((16,)), pltpu.SemaphoreType.DMA((8,)), pltpu.SemaphoreType.DMA((16,)),
+        ],
+        compiler_params=pltpu.CompilerParams(has_side_effects=True),
+        name="exchange_best")(col, row)
 
 def on_device(stream, stream_tail, archive, archive_tail):
-    r, c = lax.axis_index("row"), lax.axis_index("col")
-    nr, nc = lax.axis_size("row"), lax.axis_size("col")
-    su, au = to_unit(stream), to_unit(archive)
-    st, at = to_unit(stream_tail), to_unit(archive_tail)
-    s_blk = lax.all_gather(su, "col", axis=0, tiled=True)
-    a_blk = lax.all_gather(au, "row", axis=0, tiled=True)
-    s_head = lax.ppermute(s_blk[:31], "row", [(i, i - 1) for i in range(1, nr)])
-    a_head = lax.ppermute(a_blk[:31], "col", [(i, i - 1) for i in range(1, nc)])
-    s_head = jnp.where(r == nr - 1, st, s_head)
-    a_head = jnp.where(c == nc - 1, at, a_head)
-    u = planes(jnp.concatenate([s_blk, s_head]), C*128)
-    v = planes(jnp.concatenate([a_blk, a_head]), 4128)
+    v, u = gather(stream, stream_tail, archive, archive_tail)
     col, row = call(v, u)
-    row = row[:C].T.reshape(-1)[31:31 + 2048].reshape(16, 128)
-    row = jnp.max(lax.all_to_all(row, "col", 0, 0, tiled=True), axis=0)
-    col = jnp.max(lax.all_to_all(col, "row", 0, 0, tiled=True), axis=0)
-    return row, col
+    col, row = exchange(col, row)
+    return row.reshape(-1), col.reshape(-1)
 
 def solution(mesh):
     return jax.shard_map(

time: 244 us -> 113 us (0.46)
  waiting for transfers between devices: 146 us -> 0 us
  Pallas kernels: 48.7 us -> 110 us
  starting transfers between devices: 15.2 us -> 0 us
  between operations: 14.2 us -> 0.65 us
  other arithmetic: 13.1 us -> 0 us
  local copies, waits for them, and re-layouts: 5.21 us -> 2.39 us
    all_gather x2 -> x0, waiting for transfers between devices: 131 us -> none  [the longest x1 83.2 us: on_device(): a_blk = lax.all_gather(au, 'row', axis=0, tiled=True)]
    pallas_call x1 -> x3, Pallas kernels: 48.7 us -> 110 us  [the longest x1 49.3 us: call(): pl.pallas_call(kern, out_shape=(jax.ShapeDtypeStruct((8, 1, 512), F32), j...]
    all_to_all x2 -> x0, starting transfers between devices: 10.8 us -> none  [the longest x1 7 us: on_device(): row = jnp.max(lax.all_to_all(row, 'col', 0, 0, tiled=True), axis=0)]
    all_to_all x2 -> x0, waiting for transfers between devices: 10.2 us -> none  [the longest x1 5.68 us: on_device(): row = jnp.max(lax.all_to_all(row, 'col', 0, 0, tiled=True), axis=0)]
    ppermute x2 -> x0, waiting for transfers between devices: 4.49 us -> none  [the longest x1 3.34 us: on_device(): s_head = lax.ppermute(s_blk[:31], 'row', [(i, i - 1) for i in range(1, nr)])]
    ppermute x2 -> x0, starting transfers between devices: 4.35 us -> none  [the longest x1 3.07 us: on_device(): a_head = lax.ppermute(a_blk[:31], 'col', [(i, i - 1) for i in range(1, nc)])]
    another operation x2 -> x0, other arithmetic: 3.73 us -> none  [planes(): return jnp.stack([x[:, :128], x[:, 128:]])]
    div x2 -> x0, other arithmetic: 3.64 us -> none  [to_unit(): frames / jnp.sqrt(jnp.sum(frames * frames, axis=1, keepdims=True) + 1e-06)]
  transfers between devices with their start and end apart: 6 -> 0, of which waited for: 6 -> 0; matrix products, arithmetic and copies ran while one was open for 4% -> 0% of each run, Pallas kernels for 0% -> 0%
where the time goes in v2:
time: 113 us
  Pallas kernels  110 us (97%)
  local copies, waits for them, and re-layouts  2.39 us (2%)
    pallas_call x1, Pallas kernels, call(): pl.pallas_call(kern, out_shape=(jax.ShapeDtypeStruct((8, 1, 512), F32), j...  49.3 us
    pallas_call x1, Pallas kernels, gather(): pl.pallas_call(gather_kern, out_shape=(jax.ShapeDtypeStruct((2, 4128, 128...  43.1 us
    pallas_call x1, Pallas kernels, exchange(): pl.pallas_call(exchange_kern, out_shape=(jax.ShapeDtypeStruct((1, 512), F...  17.7 us
    unnamed x2, local copies, waits for them, and re-layouts  2.39 us

profile of v2, /device:TPU:1, one launch (start us, length us, event | category | flops | bytes accessed | tf_op | source)
XLA Modules:
  0.0 113.2 jit_solution(14498461035149438800)
XLA Ops:
  0.6 43.1 %gather_frames.1 = (f32[2,4128,128]{2,1,0:T(8,128)}, f32[2,2176,128]{2,1,0:T(8,128)}) custom-call(f32[128,256]{1,0:T(8,128)} %s_ref.1, f32[31,256]{1,0:T(8,128)} %st_ref.1, f32[512,256]{1,0:T(8,128)} %a_ref.1, f32[31,256]{1,0:T(8,128)} %at_ref.1), custom_call_target="tpu_custom_call" | custom-call | tf_op jit(solution)/shard_map/gather_frames/pallas_call | solution.py:259
  43.7 49.3 %profile_tile.1 = (f32[8,1,512]{2,1,0:T(1,128)}, f32[16,1,128]{2,1,0:T(1,128)}) custom-call(f32[2,4128,128]{2,1,0:T(8,128)} %get-tuple-element.8.v_ref, f32[2,2176,128]{2,1,0:T(8,128)} %get-tuple-element.9.u_ref), custom_call_target="tpu_custom_call" | custom-call | tf_op jit(solution)/shard_map/profile_tile/pallas_call | solution.py:121
  93.0 17.7 %exchange_best.1 = (f32[1,512]{1,0:T(1,128)}, f32[1,128]{1,0:T(1,128)}) custom-call(f32[8,1,512]{2,1,0:T(1,128)} %get-tuple-element.10.col_ref, f32[16,1,128]{2,1,0:T(1,128)} %get-tuple-element.11.row_ref), custom_call_target="tpu_custom_call" | custom-call | tf_op jit(solution)/shard_map/exchange_best/pallas_call | solution.py:301
  110.8 1.1 %copy.8 = f32[128]{0:T(128)} copy(f32[128]{0:T(128)} %bitcast.3) | data formatting | bytes 1024
  111.9 1.2 %copy.9 = f32[512]{0:T(512)} copy(f32[512]{0:T(512)} %bitcast.2) | data formatting | bytes 4096

commit v3 on v2

--- a/solution.py
+++ b/solution.py
@@ -6,88 +6,102 @@
 from jax.sharding import PartitionSpec as P
 from jax.experimental import pallas as pl
 from jax.experimental.pallas import tpu as pltpu
-M=32; C=17; SEG=512; T=544; TV=512; PAD=32
-NEG=-2.0*32
+
+M=32; C=17; SEG=512; T=544; TV=512; NB=17; BR=384
+NEG=-64.0
+DN = (((1,), (0,)), ((), ()))
+DT = (((1,), (1,)), ((), ()))
+def split(x):
+    hi = x.astype(jnp.bfloat16)
+    return hi, (x - hi.astype(jnp.float32)).astype(jnp.bfloat16)
 def prep_rhs(u_ref, b_ref):
-    def one(c,_):
-        xt = jnp.concatenate([u_ref.at[h][pl.ds(c, 128, stride=C), :].T for h in range(2)], axis=0)
-        hi = xt.astype(jnp.bfloat16)
-        lo = (xt - hi.astype(jnp.float32)).astype(jnp.bfloat16)
-        n = pl.multiple_of(c*128,128)
-        b_ref[0:256, pl.ds(n,128)] = hi
-        b_ref[256:512, pl.ds(n,128)] = lo
-        b_ref[512:768, pl.ds(n,128)] = hi
+    def one(c, _):
+        for a in range(8):
+            x = [[u_ref.at[p][pl.ds(c + 34*a + 17*h, 8, stride=272), :] for p in range(2)] for h in range(2)]
+            for w in range(3):
+                y = jnp.concatenate([jnp.concatenate(x[h], axis=1) for h in range(2)], axis=0)
+                hi, lo = split(y)
+                r = pl.multiple_of(c*BR + 16*(a + 8*w), 16)
+                b_ref[pl.ds(r, 16), 0:256] = hi
+                b_ref[pl.ds(r, 16), 256:512] = lo
+                b_ref[pl.ds(r, 16), 512:768] = hi
+                if w < 2:
+                    x = [[pltpu.roll(t, 7, 0) for t in row] for row in x]
         return 0
     lax.fori_loop(0, C, one, 0)
-def prep_lhs(v_ref, a_ref, t0, nt):
-    def one(i,_):
+def prep_lhs(v_ref, a_ref, t0, nt, unroll=8):
+    def one(i, _):
         t = t0 + i*2
-        x = jnp.concatenate([jnp.concatenate([v_ref.at[h][pl.ds(t+k, 8, stride=SEG), :] for k in range(2)], axis=0) for h in range(2)], axis=1)
-        hi = x.astype(jnp.bfloat16)
-        lo = (x - hi.astype(jnp.float32)).astype(jnp.bfloat16)
+        x = jnp.concatenate([jnp.concatenate([v_ref.at[p][pl.ds(t + d, 8, stride=SEG), :] for p in range(2)], axis=1) for d in range(2)], axis=0)
+        hi, lo = split(x)
         r = pl.multiple_of(t*8, 16)
-        a_ref[pl.ds(r,16), 0:256] = hi
-        a_ref[pl.ds(r,16), 256:512] = hi
-        a_ref[pl.ds(r,16), 512:768] = lo
+        a_ref[pl.ds(r, 16), 0:256] = hi
+        a_ref[pl.ds(r, 16), 256:512] = hi
+        a_ref[pl.ds(r, 16), 512:768] = lo
         return 0
-    lax.fori_loop(0, nt//2, one, 0, unroll=4)
-DN = (((1,), (0,)), ((), ()))
-def mm(a_ref, b_ref, g_ref, t0, nt, n, nw):
-    r = pl.multiple_of(t0*8, 16)
-    ro = pl.multiple_of((t0+PAD)*8, 16)
-    g_ref[pl.ds(ro, nt*8), pl.ds(n, nw)] = lax.dot_general(a_ref[pl.ds(r, nt*8), :], b_ref[:, pl.ds(n, nw)], DN, preferred_element_type=jnp.float32)
-def vstep(g_ref, t, E, R, tm_ref, out):
-    row = pl.multiple_of((t+PAD)*8, 8)
-    old = pl.multiple_of(t*8, 8)
-    N = []
-    for c in range(C):
-        g = g_ref[pl.ds(row,8), c*128:(c+1)*128]
-        tile, sh = (c+2, 2) if c+2 < C else (c+2-C, 1)
-        go = pltpu.roll(g_ref[pl.ds(old,8), tile*128:(tile+1)*128], sh, 1)
-        ep = E[c-1] if c else pltpu.roll(E[C-1], 1, 1)
-        N.append(ep + (g - go))
-    if out:
-        R = [jnp.maximum(r, e) for r, e in zip(R, N)]
-        mx = functools.reduce(jnp.maximum, N[5:14])
-        mb = functools.reduce(jnp.maximum, N[0:5])
-        mc = functools.reduce(jnp.maximum, N[14:17])
-        lane = lax.broadcasted_iota(jnp.int32, (8,128), 1)
-        neg = jnp.float32(NEG)
-        mid = (lane >= 2) & (lane <= 121)
-        m = jnp.where(mid, mx, neg)
-        m = jnp.maximum(m, jnp.where((lane>=2)&(lane<=122), mb, neg))
-        m = jnp.maximum(m, jnp.where((lane>=1)&(lane<=121), mc, neg))
-        tm_ref[pl.ds(pl.multiple_of((t-31)*8,8), 8), :] = m
-    return N, R
-def compute(a_ref, b_ref, g_ref, tm_ref, NT=2):
-    zero = jnp.zeros((8,128), jnp.float32)
-    g_ref[0:PAD*8, :] = jnp.zeros((PAD*8, C*128), jnp.float32)
-    lax.fori_loop(0, 8, lambda j,_: (mm(a_ref,b_ref,g_ref,0,96,pl.multiple_of(j*256,256),256),0)[1], 0)
-    mm(a_ref,b_ref,g_ref,0,96,2048,128)
-    E=[zero]*C; R=[jnp.full((8,128),NEG,jnp.float32)]*C
-    def warm(t, c):
-        n,_ = vstep(g_ref, t, list(c), R, tm_ref, False)
-        return tuple(n)
-    E = lax.fori_loop(0, 31, warm, tuple(E))
-    def blk(b, carry):
-        t0 = 96+64*b
-        def inner(j, carry):
-            E,R = list(carry[0]), list(carry[1])
-            mm(a_ref,b_ref,g_ref,t0,64,pl.multiple_of(j*256*NT,256),256*NT)
-            for k in range(8*NT):
-                E,R = vstep(g_ref, 31+64*b + j*8*NT + k, E, R, tm_ref, True)
-            return tuple(E), tuple(R)
-        carry = lax.fori_loop(0, 8//NT, inner, carry)
-        mm(a_ref,b_ref,g_ref,t0,64,2048,128)
-        return carry
-    carry = lax.fori_loop(0, 7, blk, (tuple(E),tuple(R)))
-    def fin(j, carry):
-        E,R = list(carry[0]), list(carry[1])
-        for k in range(8):
-            E,R = vstep(g_ref, 31+448 + j*8 + k, E, R, tm_ref, True)
+    lax.fori_loop(0, nt//2, one, 0, unroll=unroll)
+def mm(a_ref, b_ref, g_ref, n):
+    a = a_ref.at[pl.ds(pl.multiple_of(n*256, 256), 256), :]
+    def rows(c):
+        return b_ref[pl.ds(pl.multiple_of(c*BR + n*16, 16), 128), :]
+    for j in range(9):
+        cs = [2*j, 2*j+1] if j < 8 else [16]
+        b = jnp.concatenate([rows(c) for c in cs], axis=0)
+        g_ref[:, cs[0]*128:(cs[-1]+1)*128] = lax.dot_general(a[...], b, DT, preferred_element_type=jnp.float32)
+def seg_of(lane, n):
+    return (2*n + 2*(lane >> 4) + ((lane >> 3) & 1) + 16*(lane & 7)) & 127
+def lane_of(seg):
+    s = seg & 127
+    return ((s & 15) >> 1)*16 + (s & 1)*8 + (s >> 4)
+def take(x, idx):
+    return jnp.take_along_axis(x, idx, axis=1)
+def vblock(cur, prev, n, E, R, tm_ref, lo, hi):
+    lane = lax.broadcasted_iota(jnp.int32, (8,128), 1)
+    rel = seg_of(lane, 0)
+    prv1, nxt1, nxt2 = lane_of(rel + 127), lane_of(rel + 1), lane_of(rel + 2)
+    sg = seg_of(lane, n)
+    keepx = (sg >= 2) & (sg <= 121)
+    keepb = (sg >= 2) & (sg <= 122)
+    keepc = (sg >= 1) & (sg <= 121)
+    neg = jnp.float32(NEG)
+    E = [take(e, nxt2) for e in E]
+    R = [take(r, nxt2) for r in R]
+    for k in range(32):
+        g = lambda ref, c: ref[k*8:k*8+8, c*128:(c+1)*128]
+        N = []
+        for c in range(C):
+            old = g(prev, c+2) if c < 15 else take(g(prev, c-15), nxt1)
+            ep = E[c-1] if c else take(E[C-1], prv1)
+            N.append(ep + (g(cur, c) - old))
+        E = N
+        if lo <= k < hi:
+            R = [jnp.maximum(r, e) for r, e in zip(R, E)]
+            mx = functools.reduce(jnp.maximum, E[5:14])
+            mb = functools.reduce(jnp.maximum, E[0:5])
+            mc = functools.reduce(jnp.maximum, E[14:17])
+            m = jnp.maximum(jnp.where(keepx, mx, neg), jnp.maximum(jnp.where(keepb, mb, neg), jnp.where(keepc, mc, neg)))
+            row = (n*32 + k - 31)*8
+            tm_ref[pl.ds(pl.multiple_of(row, 8), 8), :] = m
+    return E, R
+def compute(a_ref, b_ref, gs, tm_ref):
+    z = jnp.zeros((8,128), jnp.float32)
+    E=[z]*C; R=[jnp.full((8,128), NEG, jnp.float32)]*C
+    gs[2][...] = jnp.zeros(gs[2].shape, jnp.float32)
+    mm(a_ref, b_ref, gs[0], 0)
+    mm(a_ref, b_ref, gs[1], 1)
+    E, R = vblock(gs[0], gs[2], 0, E, R, tm_ref, 31, 32)
+    def three(m, carry):
+        E, R = list(carry[0]), list(carry[1])
+        for r in range(3):
+            n = 1 + 3*m + r
+            mm(a_ref, b_ref, gs[(2+r)%3], n+1)
+            E, R = vblock(gs[(1+r)%3], gs[r%3], n, E, R, tm_ref, 0, 32)
         return tuple(E), tuple(R)
-    E,R = lax.fori_loop(0, 8, fin, carry)
-    return R
+    E, R = lax.fori_loop(0, 5, three, (tuple(E), tuple(R)))
+    E, R = vblock(gs[1], gs[0], 16, list(E), list(R), tm_ref, 0, 31)
+    lane = lax.broadcasted_iota(jnp.int32, (8,128), 1)
+    back = lane_of(lane - 32)
+    return [take(r, back) for r in R]
 def finish(tm_ref, R, col_ref, row_ref):
     def one(s, _):
         for tb in range(4):
@@ -106,11 +120,10 @@
         x = jnp.sum(x, axis=0, keepdims=True)
         for m in range(4):
             row_ref[4*j + m, 0:1, :] = x[:, 128*m:128*(m+1)]
-
-def kern(v_ref, u_ref, col_ref, row_ref, a, b, g, tm):
+def kern(v_ref, u_ref, col_ref, row_ref, a, b, g0, g1, g2, tm):
     prep_rhs(u_ref, b)
     prep_lhs(v_ref, a, 0, T)
-    R = compute(a, b, g, tm, 4)
+    R = compute(a, b, [g0, g1, g2], tm)
     finish(tm, R, col_ref, row_ref)
 
 VM = pl.BlockSpec(memory_space=pltpu.VMEM)
@@ -124,9 +137,9 @@
         in_specs=[VM, VM], out_specs=(VM, VM),
         scratch_shapes=[
             pltpu.VMEM((T*8, 768), jnp.bfloat16),
-            pltpu.VMEM((768, C*128), jnp.bfloat16),
-            pltpu.VMEM(((T+PAD)*8, C*128), jnp.float32),
-            pltpu.VMEM((TV*8, 128), jnp.float32),
+            pltpu.VMEM((C*BR, 768), jnp.bfloat16),
+            pltpu.VMEM((256, C*128), F32), pltpu.VMEM((256, C*128), F32), pltpu.VMEM((256, C*128), F32),
+            pltpu.VMEM((TV*8, 128), F32),
         ],
         compiler_params=pltpu.CompilerParams(vmem_limit_bytes=67043328),
         name="profile_tile")(v, u)

time: 113 us -> 94.1 us (0.83)
  Pallas kernels: 110 us -> 90.8 us
    pallas_call x1, Pallas kernels: 49.3 us -> 30 us  [call(): pl.pallas_call(kern, out_shape=(jax.ShapeDtypeStruct((8, 1, 512), F32), j...]
where the time goes in v3:
time: 94.1 us; the launch traced here: 93.9 us
  Pallas kernels  90.8 us (96%)
  local copies, waits for them, and re-layouts  2.39 us (3%)
    pallas_call x1, Pallas kernels, gather(): pl.pallas_call(gather_kern, out_shape=(jax.ShapeDtypeStruct((2, 4128, 128...  43.1 us
    pallas_call x1, Pallas kernels, call(): pl.pallas_call(kern, out_shape=(jax.ShapeDtypeStruct((8, 1, 512), F32), j...  30 us
    pallas_call x1, Pallas kernels, exchange(): pl.pallas_call(exchange_kern, out_shape=(jax.ShapeDtypeStruct((1, 512), F...  17.7 us
    unnamed x2, local copies, waits for them, and re-layouts  2.39 us

profile of v3, /device:TPU:1, one launch (start us, length us, event | category | flops | bytes accessed | tf_op | source)
XLA Modules:
  0.0 93.9 jit_solution(11914153223879075284)
XLA Ops:
  0.6 43.1 %gather_frames.1 = (f32[2,4128,128]{2,1,0:T(8,128)}, f32[2,2176,128]{2,1,0:T(8,128)}) custom-call(f32[128,256]{1,0:T(8,128)} %s_ref.1, f32[31,256]{1,0:T(8,128)} %st_ref.1, f32[512,256]{1,0:T(8,128)} %a_ref.1, f32[31,256]{1,0:T(8,128)} %at_ref.1), custom_call_target="tpu_custom_call" | custom-call | tf_op jit(solution)/shard_map/gather_frames/pallas_call | solution.py:272
  43.7 30.0 %profile_tile.1 = (f32[8,1,512]{2,1,0:T(1,128)}, f32[16,1,128]{2,1,0:T(1,128)}) custom-call(f32[2,4128,128]{2,1,0:T(8,128)} %get-tuple-element.8.v_ref, f32[2,2176,128]{2,1,0:T(8,128)} %get-tuple-element.9.u_ref), custom_call_target="tpu_custom_call" | custom-call | tf_op jit(solution)/shard_map/profile_tile/pallas_call | solution.py:134
  73.7 17.7 %exchange_best.1 = (f32[1,512]{1,0:T(1,128)}, f32[1,128]{1,0:T(1,128)}) custom-call(f32[8,1,512]{2,1,0:T(1,128)} %get-tuple-element.10.col_ref, f32[16,1,128]{2,1,0:T(1,128)} %get-tuple-element.11.row_ref), custom_call_target="tpu_custom_call" | custom-call | tf_op jit(solution)/shard_map/exchange_best/pallas_call | solution.py:314
  91.5 1.1 %copy.8 = f32[128]{0:T(128)} copy(f32[128]{0:T(128)} %bitcast.3) | data formatting | bytes 1024
  92.6 1.2 %copy.9 = f32[512]{0:T(512)} copy(f32[512]{0:T(512)} %bitcast.2) | data formatting | bytes 4096

commit v4 on v3

v4 whole, which is shorter than its diff:
```python
import functools

import jax
import jax.numpy as jnp
from jax import lax
from jax.sharding import PartitionSpec as P
from jax.experimental import pallas as pl
from jax.experimental.pallas import tpu as pltpu

M=32; C=17; SEG=512; T=544; TV=512; NB=17; BR=384
NEG=-64.0
DN = (((1,), (0,)), ((), ()))
DT = (((1,), (1,)), ((), ()))
def split(x):
    hi = x.astype(jnp.bfloat16)
    return hi, (x - hi.astype(jnp.float32)).astype(jnp.bfloat16)
def prep_rhs(u_ref, b_ref):
    def one(c, _):
        for a in range(8):
            x = [[u_ref.at[p][pl.ds(c + 34*a + 17*h, 8, stride=272), :] for p in range(2)] for h in range(2)]
            for w in range(3):
                y = jnp.concatenate([jnp.concatenate(x[h], axis=1) for h in range(2)], axis=0)
                hi, lo = split(y)
                r = pl.multiple_of(c*BR + 16*(a + 8*w), 16)
                b_ref[pl.ds(r, 16), 0:256] = hi
                b_ref[pl.ds(r, 16), 256:512] = lo
                b_ref[pl.ds(r, 16), 512:768] = hi
                if w < 2:
                    x = [[pltpu.roll(t, 7, 0) for t in row] for row in x]
        return 0
    lax.fori_loop(0, C, one, 0)
def prep_lhs(v_ref, a_ref, t0, nt, unroll=8):
    def one(i, _):
        t = t0 + i*2
        x = jnp.concatenate([jnp.concatenate([v_ref.at[p][pl.ds(t + d, 8, stride=SEG), :] for p in range(2)], axis=1) for d in range(2)], axis=0)
        hi, lo = split(x)
        r = pl.multiple_of(t*8, 16)
        a_ref[pl.ds(r, 16), 0:256] = hi
        a_ref[pl.ds(r, 16), 256:512] = hi
        a_ref[pl.ds(r, 16), 512:768] = lo
        return 0
    lax.fori_loop(0, nt//2, one, 0, unroll=unroll)
def mm(a_ref, b_ref, g_ref, n):
    a = a_ref.at[pl.ds(pl.multiple_of(n*256, 256), 256), :]
    def rows(c):
        return b_ref[pl.ds(pl.multiple_of(c*BR + n*16, 16), 128), :]
    for j in range(9):
        cs = [2*j, 2*j+1] if j < 8 else [16]
        b = jnp.concatenate([rows(c) for c in cs], axis=0)
        g_ref[:, cs[0]*128:(cs[-1]+1)*128] = lax.dot_general(a[...], b, DT, preferred_element_type=jnp.float32)
def seg_of(lane, n):
    return (2*n + 2*(lane >> 4) + ((lane >> 3) & 1) + 16*(lane & 7)) & 127
def lane_of(seg):
    s = seg & 127
    return ((s & 15) >> 1)*16 + (s & 1)*8 + (s >> 4)
def take(x, idx):
    return jnp.take_along_axis(x, idx, axis=1)
def vblock(cur, prev, n, E, R, tm_ref, lo, hi):
    lane = lax.broadcasted_iota(jnp.int32, (8,128), 1)
    rel = seg_of(lane, 0)
    prv1, nxt1, nxt2 = lane_of(rel + 127), lane_of(rel + 1), lane_of(rel + 2)
    sg = seg_of(lane, n)
    keepx = (sg >= 2) & (sg <= 121)
    keepb = (sg >= 2) & (sg <= 122)
    keepc = (sg >= 1) & (sg <= 121)
    neg = jnp.float32(NEG)
    E = [take(e, nxt2) for e in E]
    R = [take(r, nxt2) for r in R]
    for k in range(32):
        g = lambda ref, c: ref[k*8:k*8+8, c*128:(c+1)*128]
        N = []
        for c in range(C):
            old = g(prev, c+2) if c < 15 else take(g(prev, c-15), nxt1)
            ep = E[c-1] if c else take(E[C-1], prv1)
            N.append(ep + (g(cur, c) - old))
        E = N
        if lo <= k < hi:
            R = [jnp.maximum(r, e) for r, e in zip(R, E)]
            mx = functools.reduce(jnp.maximum, E[5:14])
            mb = functools.reduce(jnp.maximum, E[0:5])
            mc = functools.reduce(jnp.maximum, E[14:17])
            m = jnp.maximum(jnp.where(keepx, mx, neg), jnp.maximum(jnp.where(keepb, mb, neg), jnp.where(keepc, mc, neg)))
            row = (n*32 + k - 31)*8
            tm_ref[pl.ds(pl.multiple_of(row, 8), 8), :] = m
    return E, R
def compute(a_ref, b_ref, gs, tm_ref, service):
    z = jnp.zeros((8,128), jnp.float32)
    E=[z]*C; R=[jnp.full((8,128), NEG, jnp.float32)]*C
    gs[2][...] = jnp.zeros(gs[2].shape, jnp.float32)
    mm(a_ref, b_ref, gs[0], 0)
    mm(a_ref, b_ref, gs[1], 1)
    E, R = vblock(gs[0], gs[2], 0, E, R, tm_ref, 31, 32)
    def three(m, carry):
        E, R = list(carry[0]), list(carry[1])
        service(m)
        for r in range(3):
            n = 1 + 3*m + r
            mm(a_ref, b_ref, gs[(2+r)%3], n+1)
            E, R = vblock(gs[(1+r)%3], gs[r%3], n, E, R, tm_ref, 0, 32)
        return tuple(E), tuple(R)
    E, R = lax.fori_loop(0, 5, three, (tuple(E), tuple(R)))
    E, R = vblock(gs[1], gs[0], 16, list(E), list(R), tm_ref, 0, 31)
    lane = lax.broadcasted_iota(jnp.int32, (8,128), 1)
    back = lane_of(lane - 32)
    return [take(r, back) for r in R]
def finish(tm_ref, R, col_ref, row_ref):
    def one(s, _):
        for tb in range(4):
            x = tm_ref[pl.ds(s + tb*1024, 128, stride=8), :]
            col_ref[s, 0:1, tb*128:(tb+1)*128] = jnp.max(x.T, axis=0, keepdims=True)*(1.0/M)
        return 0
    lax.fori_loop(0, 8, one, 0)
    rows = jnp.concatenate([jnp.max(r, axis=0, keepdims=True) for r in R] + [jnp.full((7, 128), NEG, jnp.float32)], axis=0)*(1.0/M)
    for j in range(4):
        q = lax.broadcasted_iota(jnp.int32, (128, 512), 1) + (31 + 512*j)
        pick = (lax.broadcasted_iota(jnp.int32, (128, 512), 0) == ((q*3856) >> 16)).astype(jnp.float32)
        x = lax.dot_general(rows, pick, DN, precision=lax.Precision.HIGHEST, preferred_element_type=jnp.float32)
        q = lax.broadcasted_iota(jnp.int32, (24, 512), 1) + (31 + 512*j)
        lane = (q*3856) >> 16
        x = jnp.where(lax.broadcasted_iota(jnp.int32, (24, 512), 0) == q - lane*C, x, 0.0)
        x = jnp.sum(x, axis=0, keepdims=True)
        for m in range(4):
            row_ref[4*j + m, 0:1, :] = x[:, 128*m:128*(m+1)]
VM = pl.BlockSpec(memory_space=pltpu.VMEM)
F32 = jnp.float32
MESH = pl.DeviceIdType.MESH
NQ = 4
CH = 512 // NQ

def dev(x, y, z, k):
    return (z*2 + x % 2, (x // 2)*8 + y*2 + k)

def unit(x):
    return x / jnp.sqrt(jnp.sum(x*x, axis=1, keepdims=True) + 1e-06)

def put_planes(dst, x):
    dst[0] = x[:, :128]
    dst[1] = x[:, 128:]

def kern(s_ref, st_ref, a_ref, at_ref, colp_ref, rowp_ref, v_ref, u_ref, su, av, tails, a3, bt, g0, g1, g2, tm,
         colm, rowm, cbuf, rbuf, send, got_v, got_u, misc, csend, rsend, cgot, rgot):
    row, col = lax.axis_index("row"), lax.axis_index("col")
    z, x_lo = row // 2, row % 2
    x_hi, y, k = col // 8, (col // 2) % 4, col % 2
    x = x_hi*2 + x_lo
    home = x_lo == k
    away = x_lo != k
    cb = (x_hi*4 + y)*2 + x_lo
    rb = z*2 + k
    me_r = x_hi*8 + y*2 + x_lo
    pc, nc = (cb + 15) % 16, (cb + 1) % 16
    pr = (rb + 7) % 8
    waits, later = [], []
    count = [0]

    def remote(src, dst, sem, to, when=None, guard=None):
        c = pltpu.make_async_remote_copy(src_ref=src, dst_ref=dst, send_sem=send.at[count[0]], recv_sem=sem, device_id=to, device_id_type=MESH)
        index = count[0]
        count[0] += 1
        if guard is None:
            waits.append((c, when))
        else:
            later.append((index,) + guard)
        if when is None:
            c.start()
        else:
            pl.when(when)(c.start)

    def arrived(ref, sem):
        pltpu.make_async_copy(ref, ref, sem).wait()

    def vs(b, q):
        return v_ref.at[:, pl.ds(pl.multiple_of(b*512 + q*CH, CH), CH), :]

    def us(b, h):
        return u_ref.at[:, pl.ds(pl.multiple_of(b*128 + h*64, 64), 64), :]

    bar = pltpu.get_barrier_semaphore()

    def hello(to):
        pl.semaphore_signal(bar, inc=1, device_id=to, device_id_type=MESH)

    for c in range(2):
        for p in (1, 2, 3):
            hello(dev((x + p) % 4, y, z, c))
            hello(dev(x, (y + p) % 4, z, c))
            hello(dev(x, y, (z + p) % 4, c))
    hello(dev(x, y, z, 1 - k))
    for o in (pc, nc):
        hello(dev((o // 8)*2 + o % 2, (o // 2) % 4, z, k))
    for xx in range(4):
        for yy in range(4):
            pl.when(jnp.logical_or(away, jnp.logical_or(x != xx, y != yy)))(lambda xx=xx, yy=yy: hello(dev(xx, yy, z, x_lo)))
    for zz in range(4):
        for c in range(2):
            pl.when(jnp.logical_or(away, jnp.logical_or(z != zz, k != c)))(lambda zz=zz, c=c: hello(dev(x_hi*2 + k, y, zz, c)))

    put_planes(su, unit(s_ref[...]))
    put_planes(av, unit(a_ref[...]))
    zero = jnp.zeros((1, 256), F32)
    put_planes(tails.at[0], jnp.concatenate([unit(st_ref[...]), zero], axis=0))
    put_planes(tails.at[1], jnp.concatenate([unit(at_ref[...]), zero], axis=0))
    u_ref[:, 2080:2176, :] = jnp.zeros((2, 96, 128), F32)
    pl.when(home)(lambda: pl.semaphore_wait(bar, 43))
    pl.when(away)(lambda: pl.semaphore_wait(bar, 45))

    for h in range(2):
        src = su.at[:, pl.ds(h*64, 64), :]
        own = pltpu.make_async_copy(src, us(col, h), got_u.at[col, h])
        pl.when(home)(own.start)
        remote(src, us(col, h), got_u.at[col, h], dev(x, y, z, 1 - k), away)
        for p in (1, 3):
            remote(src, us(col, h), got_u.at[col, h], dev((x + p*k) % 4, (y + p*(1 - k)) % 4, z, x_lo))
    for q in range(NQ):
        src = av.at[:, pl.ds(q*CH, CH), :]
        local = pltpu.make_async_copy(src, vs(row, q), got_v.at[row, q])
        pl.when(home)(local.start)
        remote(src, vs(row, q), got_v.at[row, q], dev(x_hi*2 + k, y, z, 1 - k), away)
    bo = z*2 + k
    up, dn, far = (z + 1) % 4, (z + 3) % 4, (z + 2) % 4

    def ring(q):
        arrived(vs(bo, q), got_v.at[bo, q])
        for to in (dev(x, y, up, k), dev(x, y, dn, k), dev(x, y, z, 1 - k)):
            remote(vs(bo, q), vs(bo, q), got_v.at[bo, q], to)

    ring(0)
    ring(1)
    base = count[0]
    top = [0]

    def stream(flag, cols, steps):
        count[0] = base

        def blk(c, xc, dy):
            return (cols[xc] // 2)*8 + ((y + dy) % 4)*2 + c

        def get(c, xc, dy):
            b = blk(c, xc, dy)
            for h in range(2):
                arrived(us(b, h), got_u.at[b, h])

        def put(c, xc, dy, hs, to):
            b = blk(c, xc, dy)
            for h in hs:
                remote(us(b, h), us(b, h), got_u.at[b, h], to, guard=(0, flag))

        pl.when(flag)(lambda: steps(get, put))
        top[0] = max(top[0], count[0])

    def dx(p):
        return dev((x + p) % 4, y, z, k)

    def dy_(p):
        return dev(x, (y + p) % 4, z, k)

    def both(c, xc, d, to):
        return [(c, xc, d, (0, 1), t) for t in to]

    def home_steps(get, put):
        alongx, alongy = (dx(1), dx(3)), (dy_(1), dy_(3))
        for c, to in ((0, alongx), (1, alongy)):
            get(c, 0, 0)
            for o in both(c, 0, 0, to):
                put(*o)
        get(0, 0, 3)
        put(0, 0, 3, (0,), dy_(1))
        for o in both(0, 0, 3, alongx):
            put(*o)
        get(0, 0, 1)
        put(0, 0, 1, (1,), dy_(3))
        for o in both(0, 0, 1, alongx):
            put(*o)
        get(1, 1, 0)
        for o in both(1, 1, 0, alongy):
            put(*o)
        get(0, 0, 2)
        for o in both(0, 0, 2, alongx):
            put(*o)
        for xc in range(2):
            get(1, xc, 3)
            put(1, xc, 3, (0,), dy_(1))
            get(1, xc, 1)
            put(1, xc, 1, (1,), dy_(3))
        for xc in range(2):
            get(1, xc, 2)
        for d in range(4):
            get(0, 1, d)

    def away_steps(get, put):
        alongy = (dy_(1), dy_(3))
        get(1, 0, 0)
        put(1, 0, 0, (0,), dx(1))
        for o in both(1, 0, 0, alongy):
            put(*o)
        get(1, 1, 0)
        put(1, 1, 0, (1,), dx(3))
        for o in both(1, 1, 0, alongy):
            put(*o)

        def relay(d):
            get(0, 0, d)
            put(0, 0, d, (0,), dx(1))
            get(0, 1, d)
            put(0, 1, d, (1,), dx(3))

        relay(0)
        for xc in range(2):
            get(1, xc, 3)
            put(1, xc, 3, (0,), dy_(1))
            get(1, xc, 1)
            put(1, xc, 1, (1,), dy_(3))
        relay(3)
        relay(1)
        relay(2)
        for xc in range(2):
            get(1, xc, 2)

    stream(home, (x, (x + 2) % 4), home_steps)
    stream(away, ((x + 3) % 4, (x + 1) % 4), away_steps)
    count[0] = top[0]
    ring(2)
    ring(3)
    remote(u_ref.at[:, pl.ds(0, 32), :], u_ref.at[:, pl.ds(2048, 32), :], misc.at[0], dev(x, y, pr // 2, pr % 2), rb != 0)
    tu = pltpu.make_async_copy(tails.at[0], u_ref.at[:, pl.ds(2048, 32), :], misc.at[0])
    pl.when(rb == 7)(tu.start)
    bu, bd, bf = up*2 + k, dn*2 + k, far*2 + k

    def near(q):
        for b, to, turn in ((bd, up, 0), (bu, dn, 1)):
            arrived(vs(b, q), got_v.at[b, q])
            if q % 2 == turn:
                remote(vs(b, q), vs(b, q), got_v.at[b, q], dev(x, y, to, k))
            remote(vs(b, q), vs(b, q), got_v.at[b, q], dev(x, y, z, 1 - k))

    def distant(q):
        arrived(vs(bf, q), got_v.at[bf, q])
        remote(vs(bf, q), vs(bf, q), got_v.at[bf, q], dev(x, y, z, 1 - k), guard=(0,))

    def others(q):
        for zz in range(4):
            b = zz*2 + 1 - k
            arrived(vs(b, q), got_v.at[b, q])

    for q in range(NQ):
        near(q)
    tu.wait()
    prep_rhs(u_ref, bt)
    distant(0)
    distant(1)
    others(0)
    remote(v_ref.at[:, pl.ds(0, 32), :], v_ref.at[:, pl.ds(4096, 32), :], misc.at[1], dev((pc // 8)*2 + pc % 2, (pc // 2) % 4, z, k), cb != 0)
    tv = pltpu.make_async_copy(tails.at[1], v_ref.at[:, pl.ds(4096, 32), :], misc.at[1])
    pl.when(cb == 15)(tv.start)
    others(1)
    prep_lhs(v_ref, a3, 0, 256)

    def service(m):
        def early():
            distant(2)
            distant(3)

        def third():
            others(2)
            prep_lhs(v_ref, a3, 256, 128)

        def fourth():
            others(3)
            prep_lhs(v_ref, a3, 384, 128)

        def last():
            tv.wait()
            prep_lhs(v_ref, a3, 512, 32)

        pl.when(m == 1)(early)
        pl.when(m == 2)(third)
        pl.when(m == 3)(fourth)
        pl.when(m == 4)(last)

    R = compute(a3, bt, [g0, g1, g2], tm, service)
    finish(tm, R, colm, rowm)
    for c, when in waits:
        if when is None:
            c.wait_send()
        else:
            pl.when(when)(c.wait_send)
    for index, *how in later:
        if len(how) == 1:
            arrived(vs(0, 0), send.at[index])
        else:
            pl.when(how[1])(lambda index=index: arrived(us(0, 0), send.at[index]))
    cp = []
    for s in range(8):
        other = jnp.logical_or(row != s, away)
        c = pltpu.make_async_remote_copy(src_ref=colm.at[s], dst_ref=cbuf.at[rb], send_sem=csend.at[s], recv_sem=cgot.at[rb], device_id=(s, me_r), device_id_type=MESH)
        pl.when(other)(c.start)
        cp.append((c, other))
    for j in range(16):
        other = jnp.logical_or(col != j, away)
        c = pltpu.make_async_remote_copy(src_ref=rowm.at[j], dst_ref=rbuf.at[me_r], send_sem=rsend.at[j], recv_sem=rgot.at[me_r], device_id=(rb, j), device_id_type=MESH)
        pl.when(other)(c.start)
        cp.append((c, other))
    lc = pltpu.make_async_copy(colm.at[row], cbuf.at[rb], cgot.at[rb])
    lr = pltpu.make_async_copy(rowm.at[col], rbuf.at[me_r], rgot.at[me_r])
    pl.when(home)(lc.start)
    pl.when(home)(lr.start)
    for s in range(8):
        arrived(cbuf.at[s], cgot.at[s])
    for j in range(16):
        arrived(rbuf.at[j], rgot.at[j])
    colp_ref[...] = functools.reduce(jnp.maximum, [cbuf[s] for s in range(8)])
    rowp_ref[...] = functools.reduce(jnp.maximum, [rbuf[j] for j in range(16)])
    for c, other in cp:
        pl.when(other)(c.wait_send)

def on_device(stream, stream_tail, archive, archive_tail):
    DMA = pltpu.SemaphoreType.DMA
    col, row = pl.pallas_call(
        kern,
        out_shape=(jax.ShapeDtypeStruct((1, 512), F32), jax.ShapeDtypeStruct((1, 128), F32)),
        in_specs=[VM]*4, out_specs=(VM, VM),
        scratch_shapes=[
            pltpu.VMEM((2, 4128, 128), F32), pltpu.VMEM((2, 2176, 128), F32),
            pltpu.VMEM((2, 128, 128), F32), pltpu.VMEM((2, 512, 128), F32), pltpu.VMEM((2, 2, 32, 128), F32),
            pltpu.VMEM((T*8, 768), jnp.bfloat16), pltpu.VMEM((C*BR, 768), jnp.bfloat16),
            pltpu.VMEM((256, C*128), F32), pltpu.VMEM((256, C*128), F32), pltpu.VMEM((256, C*128), F32),
            pltpu.VMEM((TV*8, 128), F32),
            pltpu.VMEM((8, 1, 512), F32), pltpu.VMEM((16, 1, 128), F32),
            pltpu.VMEM((8, 1, 512), F32), pltpu.VMEM((16, 1, 128), F32),
            DMA((100,)), DMA((8, NQ)), DMA((16, 2)), DMA((2,)),
            DMA((8,)), DMA((16,)), DMA((8,)), DMA((16,)),
        ],
        compiler_params=pltpu.CompilerParams(has_side_effects=True, collective_id=0, vmem_limit_bytes=67043328),
        name="join_profile")(stream, stream_tail, archive, archive_tail)
    return row.reshape(-1), col.reshape(-1)

def solution(mesh):
    return jax.shard_map(
        on_device, mesh=mesh,
        in_specs=(P(("row", "col"), None), P(), P(("col", "row"), None), P()),
        out_specs=(P(("row", "col")), P(("col", "row"))),
        check_vma=False)
```

time: 94.1 us -> 77.7 us (0.83)
  Pallas kernels: 90.8 us -> 75.2 us
    pallas_call x3 -> x1, Pallas kernels: 90.8 us -> 75.2 us  [on_device(): pl.pallas_call(kern, out_shape=(jax.ShapeDtypeStruct((1, 512), F32), jax....]
    unnamed x2 -> x6, local copies, waits for them, and re-layouts: 2.39 us -> 1.71 us
where the time goes in v4:
time: 77.7 us; the launch traced here: 77.6 us
  Pallas kernels  75.2 us (97%)
  local copies, waits for them, and re-layouts  1.71 us (2%)
    pallas_call x1, Pallas kernels, on_device(): pl.pallas_call(kern, out_shape=(jax.ShapeDtypeStruct((1, 512), F32), jax....  75.2 us
    unnamed x6, local copies, waits for them, and re-layouts  1.71 us

profile of v4, /device:TPU:1, one launch (start us, length us, event | category | flops | bytes accessed | tf_op | source)
XLA Modules:
  0.0 77.6 jit_solution(2854400405613526141)
XLA Ops:
  0.6 75.2 %join_profile.1 = (f32[1,512]{1,0:T(1,128)}, f32[1,128]{1,0:T(1,128)}) custom-call(f32[128,256]{1,0:T(8,128)} %s_ref.1, f32[31,256]{1,0:T(8,128)} %st_ref.1, f32[512,256]{1,0:T(8,128)} %a_ref.1, f32[31,256]{1,0:T(8,128)} %at_ref.1), custom_call_target="tpu_custom_call" | custom-call | tf_op jit(solution)/shard_map/join_profile/pallas_call | solution.py:418
  75.8 0.0 copy-start.1
  75.9 0.0 copy-start
  75.9 0.6 copy-done.1
  76.5 0.5 copy.8
  77.0 0.0 copy-done
  77.0 0.6 copy.9
Async XLA Ops:
  75.8 0.6 copy-start.1
  75.9 1.1 %copy-start = (f32[1,512]{1,0:T(1,128)S(1)}, f32[1,512]{1,0:T(1,128)}, u32[]{:S(2)}) copy-start(f32[1,512]{1,0:T(1,128)} %get-tuple-element.5) | copy-start | bytes 6148

commit v5 on v4

v5 whole, which is shorter than its diff:
```python
import functools

import jax
import jax.numpy as jnp
from jax import lax
from jax.sharding import PartitionSpec as P
from jax.experimental import pallas as pl
from jax.experimental.pallas import tpu as pltpu

M=32; C=17; SEGR=544; T=544; TV=512; NB=17; BR=384
NEG=-64.0
DN = (((1,), (0,)), ((), ()))
DT = (((1,), (1,)), ((), ()))
def split(x):
    hi = x.astype(jnp.bfloat16)
    return hi, (x - hi.astype(jnp.float32)).astype(jnp.bfloat16)
def prep_rhs(u_ref, b_ref):
    def one(c, _):
        for a in range(8):
            x = [[u_ref.at[p][pl.ds(c + 34*a + 17*h, 8, stride=272), :] for p in range(2)] for h in range(2)]
            for w in range(3):
                y = jnp.concatenate([jnp.concatenate(x[h], axis=1) for h in range(2)], axis=0)
                hi, lo = split(y)
                r = pl.multiple_of(c*BR + 16*(a + 8*w), 16)
                b_ref[pl.ds(r, 16), 0:256] = hi
                b_ref[pl.ds(r, 16), 256:512] = lo
                b_ref[pl.ds(r, 16), 512:768] = hi
                if w < 2:
                    x = [[pltpu.roll(t, 7, 0) for t in row] for row in x]
        return 0
    lax.fori_loop(0, C, one, 0)
def prep_lhs(v_ref, a_ref, n):
    for i in range(16):
        x = jnp.concatenate([jnp.concatenate([v_ref.at[p][pl.ds(n*32 + 2*i + d, 8, stride=SEGR), :] for p in range(2)], axis=1) for d in range(2)], axis=0)
        hi, lo = split(x)
        a_ref[16*i:16*i+16, 0:256] = hi
        a_ref[16*i:16*i+16, 256:512] = hi
        a_ref[16*i:16*i+16, 512:768] = lo
def mm(a_ref, b_ref, g_ref, n):
    def rows(c):
        return b_ref[pl.ds(pl.multiple_of(c*BR + n*16, 16), 128), :]
    for j in range(9):
        cs = [2*j, 2*j+1] if j < 8 else [16]
        b = jnp.concatenate([rows(c) for c in cs], axis=0)
        g_ref[:, cs[0]*128:(cs[-1]+1)*128] = lax.dot_general(a_ref[...], b, DT, preferred_element_type=jnp.float32)
def seg_of(lane, n):
    return (2*n + 2*(lane >> 4) + ((lane >> 3) & 1) + 16*(lane & 7)) & 127
def lane_of(seg):
    s = seg & 127
    return ((s & 15) >> 1)*16 + (s & 1)*8 + (s >> 4)
def take(x, idx):
    return jnp.take_along_axis(x, idx, axis=1)
def vblock(cur, prev, n, E, R, acc_ref, lo, hi):
    lane = lax.broadcasted_iota(jnp.int32, (8,128), 1)
    rel = seg_of(lane, 0)
    prv1, nxt1, nxt2 = lane_of(rel + 127), lane_of(rel + 1), lane_of(rel + 2)
    sg = seg_of(lane, n)
    keepx = (sg >= 2) & (sg <= 121)
    keepb = (sg >= 2) & (sg <= 122)
    keepc = (sg >= 1) & (sg <= 121)
    neg = jnp.float32(NEG)
    acc = jnp.full((8, 128), NEG, jnp.float32)
    spot = (n & 3)*32
    E = [take(e, nxt2) for e in E]
    R = [take(r, nxt2) for r in R]
    for k in range(32):
        g = lambda ref, c: ref[k*8:k*8+8, c*128:(c+1)*128]
        N = []
        for c in range(C):
            old = g(prev, c+2) if c < 15 else take(g(prev, c-15), nxt1)
            ep = E[c-1] if c else take(E[C-1], prv1)
            N.append(ep + (g(cur, c) - old))
        E = N
        if lo <= k < hi:
            R = [jnp.maximum(r, e) for r, e in zip(R, E)]
            mx = functools.reduce(jnp.maximum, E[5:14])
            mb = functools.reduce(jnp.maximum, E[0:5])
            mc = functools.reduce(jnp.maximum, E[14:17])
            m = jnp.maximum(jnp.where(keepx, mx, neg), jnp.maximum(jnp.where(keepb, mb, neg), jnp.where(keepc, mc, neg)))
            acc = jnp.where(lane == spot + k, jnp.max(m, axis=1, keepdims=True), acc)
    tile = acc_ref.at[:, pl.ds(pl.multiple_of((n >> 2)*128, 128), 128)]
    tile[...] = jnp.where((lane >> 5) == (n & 3), acc, tile[...])
    return E, R
def compute(v_ref, a, b_ref, gs, acc_ref, service):
    z = jnp.zeros((8,128), jnp.float32)
    E = [z]*C
    R = [jnp.full((8,128), NEG, jnp.float32)]*C
    gs[2][...] = jnp.zeros(gs[2].shape, jnp.float32)
    first = jnp.int32(0)
    for n in range(3):
        prep_lhs(v_ref, a[n], n)
    mm(a[0], b_ref, gs[0], 0)
    mm(a[1], b_ref, gs[1], 1)
    E, R = vblock(gs[0], gs[2], first, E, R, acc_ref, 31, 32)
    def three(m, carry):
        E, R = list(carry[0]), list(carry[1])
        service(m)
        for r in range(3):
            n = 1 + 3*m + r
            mm(a[(2+r)%3], b_ref, gs[(2+r)%3], n+1)
            prep_lhs(v_ref, a[r%3], jnp.minimum(n+2, NB-1))
            E, R = vblock(gs[(1+r)%3], gs[r%3], n, E, R, acc_ref, 0, 32)
        return tuple(E), tuple(R)
    E, R = lax.fori_loop(0, 5, three, (tuple(E), tuple(R)))
    E, R = vblock(gs[1], gs[0], first + 16, list(E), list(R), acc_ref, 0, 31)
    lane = lax.broadcasted_iota(jnp.int32, (8,128), 1)
    back = lane_of(lane - 32)
    return [take(r, back) for r in R]
def finish(acc_ref, R, col_ref, row_ref):
    lane = lax.broadcasted_iota(jnp.int32, (8, 128), 1)
    turned = [pltpu.roll(acc_ref[:, 128*j:128*(j+1)], 97, 1) for j in range(5)]
    for j in range(4):
        best = jnp.where(lane < 97, turned[j], turned[j+1])*(1.0/M)
        for s in range(8):
            col_ref[s, 0:1, 128*j:128*(j+1)] = best[s:s+1]
    rows = jnp.concatenate([jnp.max(r, axis=0, keepdims=True) for r in R] + [jnp.full((7, 128), NEG, jnp.float32)], axis=0)*(1.0/M)
    for j in range(4):
        q = lax.broadcasted_iota(jnp.int32, (128, 512), 1) + (31 + 512*j)
        pick = (lax.broadcasted_iota(jnp.int32, (128, 512), 0) == ((q*3856) >> 16)).astype(jnp.float32)
        x = lax.dot_general(rows, pick, DN, precision=lax.Precision.HIGHEST, preferred_element_type=jnp.float32)
        q = lax.broadcasted_iota(jnp.int32, (24, 512), 1) + (31 + 512*j)
        lane = (q*3856) >> 16
        x = jnp.where(lax.broadcasted_iota(jnp.int32, (24, 512), 0) == q - lane*C, x, 0.0)
        x = jnp.sum(x, axis=0, keepdims=True)
        for m in range(4):
            row_ref[4*j + m, 0:1, :] = x[:, 128*m:128*(m+1)]
VM = pl.BlockSpec(memory_space=pltpu.VMEM)
F32 = jnp.float32
MESH = pl.DeviceIdType.MESH
NQ = 4
CH = SEGR // NQ

def dev(x, y, z, k):
    return (z*2 + x % 2, (x // 2)*8 + y*2 + k)

def unit(x):
    return x * (1.0 / jnp.sqrt(jnp.sum(x*x, axis=1, keepdims=True) + 1e-06))

def put_planes(dst, x):
    dst[0] = x[:, :128]
    dst[1] = x[:, 128:]

def kern(s_ref, st_ref, a_ref, at_ref, colp_ref, rowp_ref, v_ref, u_ref, su, tails, a0, a1, a2, bt, g0, g1, g2, acc,
         colm, rowm, cbuf, rbuf, send, got_v, got_u, misc, csend, rsend, cgot, rgot):
    row, col = lax.axis_index("row"), lax.axis_index("col")
    z, x_lo = row // 2, row % 2
    x_hi, y, k = col // 8, (col // 2) % 4, col % 2
    x = x_hi*2 + x_lo
    home = x_lo == k
    away = x_lo != k
    rb = z*2 + k
    me_r = x_hi*8 + y*2 + x_lo
    blk_no = col*8 + row
    pb, nb = (blk_no + 127) % 128, (blk_no + 1) % 128
    pr = (rb + 7) % 8
    waits, later = [], []
    count = [0]

    def remote(src, dst, sem, to, when=None, guard=None):
        c = pltpu.make_async_remote_copy(src_ref=src, dst_ref=dst, send_sem=send.at[count[0]], recv_sem=sem, device_id=to, device_id_type=MESH)
        index = count[0]
        count[0] += 1
        if guard is None:
            waits.append((c, when))
        else:
            later.append((index,) + guard)
        if when is None:
            c.start()
        else:
            pl.when(when)(c.start)

    def arrived(ref, sem):
        pltpu.make_async_copy(ref, ref, sem).wait()

    def vs(b, q):
        return v_ref.at[:, pl.ds(pl.multiple_of(b*SEGR + q*CH, 8), CH), :]

    def us(b, h):
        return u_ref.at[:, pl.ds(pl.multiple_of(b*128 + h*64, 64), 64), :]

    bar = pltpu.get_barrier_semaphore()

    def hello(to):
        pl.semaphore_signal(bar, inc=1, device_id=to, device_id_type=MESH)

    for c in range(2):
        for p in (1, 2, 3):
            hello(dev((x + p) % 4, y, z, c))
            hello(dev(x, (y + p) % 4, z, c))
            hello(dev(x, y, (z + p) % 4, c))
    hello(dev(x, y, z, 1 - k))
    for o in (pb, nb):
        hello((o % 8, o // 8))
    for xx in range(4):
        for yy in range(4):
            pl.when(jnp.logical_or(away, jnp.logical_or(x != xx, y != yy)))(lambda xx=xx, yy=yy: hello(dev(xx, yy, z, x_lo)))

    put_planes(su, unit(s_ref[...]))
    u_ref[:, 2080:2176, :] = jnp.zeros((2, 96, 128), F32)
    zero = jnp.zeros((1, 256), F32)
    put_planes(tails.at[0], jnp.concatenate([unit(st_ref[...]), zero], axis=0))
    put_planes(tails.at[1], jnp.concatenate([unit(at_ref[...]), zero], axis=0))
    pl.when(home)(lambda: pl.semaphore_wait(bar, 36))
    pl.when(away)(lambda: pl.semaphore_wait(bar, 37))

    for h in range(2):
        src = su.at[:, pl.ds(h*64, 64), :]
        own = pltpu.make_async_copy(src, us(col, h), got_u.at[col, h])
        pl.when(home)(own.start)
        remote(src, us(col, h), got_u.at[col, h], dev(x, y, z, 1 - k), away)
        for p in (1, 3):
            remote(src, us(col, h), got_u.at[col, h], dev((x + p*k) % 4, (y + p*(1 - k)) % 4, z, x_lo))
    up, dn, far = (z + 1) % 4, (z + 3) % 4, (z + 2) % 4
    bo = z*2 + k
    put_planes(v_ref.at[:, pl.ds(pl.multiple_of(bo*SEGR, 8), 512), :], unit(a_ref[...]))
    head = v_ref.at[:, pl.ds(pl.multiple_of(bo*SEGR, 8), 32), :]
    pz, pk = (pb % 8) // 2, (pb // 8) % 2
    remote(head, v_ref.at[:, pl.ds(pl.multiple_of((pz*2 + pk)*SEGR + 512, 8), 32), :], misc.at[1], (pb % 8, pb // 8), blk_no != 0)
    halo = v_ref.at[:, pl.ds(pl.multiple_of(bo*SEGR + 512, 8), 32), :]
    tv = pltpu.make_async_copy(tails.at[1], halo, misc.at[1])
    pl.when(blk_no == 127)(tv.start)

    def ring(q):
        for to in (dev(x, y, up, k), dev(x, y, dn, k), dev(x, y, z, 1 - k)):
            remote(vs(bo, q), vs(bo, q), got_v.at[bo, q], to)

    ring(0)
    ring(1)
    bu, bd, bf = up*2 + k, dn*2 + k, far*2 + k

    def near(q):
        for b, to, turn in ((bd, up, 0), (bu, dn, 1)):
            arrived(vs(b, q), got_v.at[b, q])
            if q % 2 == turn:
                remote(vs(b, q), vs(b, q), got_v.at[b, q], dev(x, y, to, k), guard=(0,))
            remote(vs(b, q), vs(b, q), got_v.at[b, q], dev(x, y, z, 1 - k), guard=(0,))

    def distant(q):
        arrived(vs(bf, q), got_v.at[bf, q])
        remote(vs(bf, q), vs(bf, q), got_v.at[bf, q], dev(x, y, z, 1 - k), guard=(0,))

    def others(q):
        for zz in range(4):
            b = zz*2 + 1 - k
            arrived(vs(b, q), got_v.at[b, q])

    def next_rows():
        pltpu.make_async_remote_copy(src_ref=u_ref.at[:, pl.ds(0, 32), :], dst_ref=u_ref.at[:, pl.ds(2048, 32), :], send_sem=misc.at[2], recv_sem=misc.at[0], device_id=dev(x, y, pr // 2, pr % 2), device_id_type=MESH).start()

    def stream(flag, cols, step):
        def blk(c, xc, d):
            return (cols[xc] // 2)*8 + ((y + d) % 4)*2 + c

        def get(c, xc, d):
            b = blk(c, xc, d)
            for h in range(2):
                arrived(us(b, h), got_u.at[b, h])
            if c == 0:
                pl.when(jnp.logical_and(b == 0, rb != 0))(next_rows)

        def put(c, xc, d, hs, *targets):
            b = blk(c, xc, d)
            for to in targets:
                for h in hs:
                    remote(us(b, h), us(b, h), got_u.at[b, h], to, guard=(0, flag))

        pl.when(flag)(lambda: step(get, put))

    def dx(p):
        return dev((x + p) % 4, y, z, k)

    def dy(p):
        return dev(x, (y + p) % 4, z, k)

    full = (0, 1)

    def h0(get, put):
        get(0, 0, 0)
        put(0, 0, 0, full, dx(1), dx(3))
        get(1, 0, 0)
        put(1, 0, 0, full, dy(1), dy(3))

    def h1(get, put):
        get(0, 0, 3)
        put(0, 0, 3, (0,), dy(1))
        put(0, 0, 3, full, dx(1), dx(3))
        get(0, 0, 1)
        put(0, 0, 1, (1,), dy(3))
        put(0, 0, 1, full, dx(1), dx(3))

    def h2(get, put):
        get(1, 1, 0)
        put(1, 1, 0, full, dy(1), dy(3))
        get(0, 0, 2)
        put(0, 0, 2, full, dx(1), dx(3))

    def yrelay(xc):
        def step(get, put):
            get(1, xc, 3)
            put(1, xc, 3, (0,), dy(1))
            get(1, xc, 1)
            put(1, xc, 1, (1,), dy(3))
        return step

    def h5(get, put):
        for xc in range(2):
            get(1, xc, 2)
        for d in range(4):
            get(0, 1, d)

    def away0(get, put):
        get(1, 0, 0)
        put(1, 0, 0, (0,), dx(1))
        put(1, 0, 0, full, dy(1), dy(3))
        get(1, 1, 0)
        put(1, 1, 0, (1,), dx(3))
        put(1, 1, 0, full, dy(1), dy(3))

    def away1(*ds):
        def step(get, put):
            for d in ds:
                get(0, 0, d)
                put(0, 0, d, (0,), dx(1))
                get(0, 1, d)
                put(0, 1, d, (1,), dx(3))
        return step

    def a5(get, put):
        for xc in range(2):
            get(1, xc, 2)

    hc = (x, (x + 2) % 4)
    ac = ((x + 3) % 4, (x + 1) % 4)

    def H(step):
        stream(home, hc, step)

    def A(step):
        stream(away, ac, step)

    H(h0)
    A(away0)
    near(0)
    ring(2)
    H(h1)
    A(away1(0))
    H(h2)
    A(yrelay(0))
    A(yrelay(1))
    near(1)
    tv.wait()
    ring(3)
    H(yrelay(0))
    A(away1(3))
    A(away1(1))
    H(yrelay(1))
    A(away1(2))
    H(h5)
    A(a5)
    tu = pltpu.make_async_copy(tails.at[0], u_ref.at[:, pl.ds(2048, 32), :], misc.at[0])
    pl.when(rb == 7)(tu.start)
    distant(0)
    distant(1)
    tu.wait()
    prep_rhs(u_ref, bt)
    others(0)
    near(2)
    others(1)

    def service(m):
        def first():
            near(3)
            distant(2)

        def third():
            distant(3)

        pl.when(m == 0)(first)
        pl.when(m == 1)(lambda: others(2))
        pl.when(m == 2)(third)
        pl.when(m == 3)(lambda: others(3))

    acc[...] = jnp.full(acc.shape, NEG, F32)
    R = compute(v_ref, [a0, a1, a2], bt, [g0, g1, g2], acc, service)
    finish(acc, R, colm, rowm)
    for c, when in waits:
        if when is None:
            c.wait_send()
        else:
            pl.when(when)(c.wait_send)
    pl.when(rb != 0)(lambda: arrived(u_ref.at[:, pl.ds(0, 32), :], misc.at[2]))
    for index, *how in later:
        if len(how) == 1:
            arrived(vs(0, 0), send.at[index])
        else:
            pl.when(how[1])(lambda index=index: arrived(us(0, 0), send.at[index]))
    cp = []
    for s in range(8):
        other = rb != s
        c = pltpu.make_async_remote_copy(src_ref=colm.at[s], dst_ref=cbuf.at[rb], send_sem=csend.at[s], recv_sem=cgot.at[rb], device_id=dev(x, y, s // 2, s % 2), device_id_type=MESH)
        pl.when(other)(c.start)
        cp.append((c, other))
    for j in range(16):
        other = jnp.logical_or(col != j, away)
        c = pltpu.make_async_remote_copy(src_ref=rowm.at[j], dst_ref=rbuf.at[me_r], send_sem=rsend.at[j], recv_sem=rgot.at[me_r], device_id=(rb, j), device_id_type=MESH)
        pl.when(other)(c.start)
        cp.append((c, other))
    lc = pltpu.make_async_copy(colm.at[rb], cbuf.at[rb], cgot.at[rb])
    lr = pltpu.make_async_copy(rowm.at[col], rbuf.at[me_r], rgot.at[me_r])
    lc.start()
    pl.when(home)(lr.start)
    for s in range(8):
        arrived(cbuf.at[s], cgot.at[s])
    for j in range(16):
        arrived(rbuf.at[j], rgot.at[j])
    colp_ref[...] = functools.reduce(jnp.maximum, [cbuf[s] for s in range(8)])
    rowp_ref[...] = functools.reduce(jnp.maximum, [rbuf[j] for j in range(16)])
    for c, other in cp:
        pl.when(other)(c.wait_send)

def on_device(stream, stream_tail, archive, archive_tail):
    DMA = pltpu.SemaphoreType.DMA
    col, row = pl.pallas_call(
        kern,
        out_shape=(jax.ShapeDtypeStruct((1, 512), F32), jax.ShapeDtypeStruct((1, 128), F32)),
        in_specs=[VM]*4, out_specs=(VM, VM),
        scratch_shapes=[
            pltpu.VMEM((2, 8*SEGR, 128), F32), pltpu.VMEM((2, 2176, 128), F32),
            pltpu.VMEM((2, 128, 128), F32), pltpu.VMEM((2, 2, 32, 128), F32),
            pltpu.VMEM((256, 768), jnp.bfloat16), pltpu.VMEM((256, 768), jnp.bfloat16), pltpu.VMEM((256, 768), jnp.bfloat16), pltpu.VMEM((C*BR, 768), jnp.bfloat16),
            pltpu.VMEM((256, C*128), F32), pltpu.VMEM((256, C*128), F32), pltpu.VMEM((256, C*128), F32),
            pltpu.VMEM((8, 640), F32),
            pltpu.VMEM((8, 1, 512), F32), pltpu.VMEM((16, 1, 128), F32),
            pltpu.VMEM((8, 1, 512), F32), pltpu.VMEM((16, 1, 128), F32),
            DMA((140,)), DMA((8, NQ)), DMA((16, 2)), DMA((3,)),
            DMA((8,)), DMA((16,)), DMA((8,)), DMA((16,)),
        ],
        compiler_params=pltpu.CompilerParams(has_side_effects=True, collective_id=0, vmem_limit_bytes=67043328),
        name="join_profile")(stream, stream_tail, archive, archive_tail)
    return row.reshape(-1), col.reshape(-1)

def solution(mesh):
    return jax.shard_map(
        on_device, mesh=mesh,
        in_specs=(P(("row", "col"), None), P(), P(("col", "row"), None), P()),
        out_specs=(P(("row", "col")), P(("col", "row"))),
        check_vma=False)
```

time: 77.7 us -> 66.1 us (0.85)
  Pallas kernels: 75.2 us -> 63.6 us
    pallas_call x1, Pallas kernels: 75.2 us -> 63.6 us  [on_device(): pl.pallas_call(kern, out_shape=(jax.ShapeDtypeStruct((1, 512), F32), jax....]
where the time goes in v5:
time: 66.1 us; the launch traced here: 66 us
  Pallas kernels  63.6 us (96%)
  local copies, waits for them, and re-layouts  1.71 us (3%)
    pallas_call x1, Pallas kernels, on_device(): pl.pallas_call(kern, out_shape=(jax.ShapeDtypeStruct((1, 512), F32), jax....  63.6 us
    unnamed x6, local copies, waits for them, and re-layouts  1.71 us

profile of v5, /device:TPU:1, one launch (start us, length us, event | category | flops | bytes accessed | tf_op | source)
XLA Modules:
  0.0 66.0 jit_solution(8517568686363125667)
XLA Ops:
  0.6 63.6 %join_profile.1 = (f32[1,512]{1,0:T(1,128)}, f32[1,128]{1,0:T(1,128)}) custom-call(f32[128,256]{1,0:T(8,128)} %s_ref.1, f32[31,256]{1,0:T(8,128)} %st_ref.1, f32[512,256]{1,0:T(8,128)} %a_ref.1, f32[31,256]{1,0:T(8,128)} %at_ref.1), custom_call_target="tpu_custom_call" | custom-call | tf_op jit(solution)/shard_map/join_profile/pallas_call | solution.py:423
  64.2 0.0 copy-start.1
  64.2 0.0 copy-start
  64.3 0.6 copy-done.1
  64.9 0.5 copy.8
  65.4 0.0 copy-done
  65.4 0.6 copy.9
Async XLA Ops:
  64.2 0.6 copy-start.1
  64.2 1.1 %copy-start = (f32[1,512]{1,0:T(1,128)S(1)}, f32[1,512]{1,0:T(1,128)}, u32[]{:S(2)}) copy-start(f32[1,512]{1,0:T(1,128)} %get-tuple-element.5) | copy-start | bytes 6148

commit v6 on v5

--- a/solution.py
+++ b/solution.py
@@ -11,35 +11,39 @@
 NEG=-64.0
 DN = (((1,), (0,)), ((), ()))
 DT = (((1,), (1,)), ((), ()))
-def split(x):
+S = 32.0
+def split_left(x):
     hi = x.astype(jnp.bfloat16)
-    return hi, (x - hi.astype(jnp.float32)).astype(jnp.bfloat16)
+    top = hi.astype(jnp.float32)
+    return hi, (top + S*(x - top)).astype(jnp.bfloat16)
+def split_right(y):
+    most = y*(1.0 - 1.0/S)
+    hi = most.astype(jnp.bfloat16)
+    return hi, (y*(1.0/S) + (most - hi.astype(jnp.float32))).astype(jnp.bfloat16)
 def prep_rhs(u_ref, b_ref):
     def one(c, _):
         for a in range(8):
             x = [[u_ref.at[p][pl.ds(c + 34*a + 17*h, 8, stride=272), :] for p in range(2)] for h in range(2)]
             for w in range(3):
                 y = jnp.concatenate([jnp.concatenate(x[h], axis=1) for h in range(2)], axis=0)
-                hi, lo = split(y)
+                hi, lo = split_right(y)
                 r = pl.multiple_of(c*BR + 16*(a + 8*w), 16)
                 b_ref[pl.ds(r, 16), 0:256] = hi
                 b_ref[pl.ds(r, 16), 256:512] = lo
-                b_ref[pl.ds(r, 16), 512:768] = hi
                 if w < 2:
                     x = [[pltpu.roll(t, 7, 0) for t in row] for row in x]
         return 0
     lax.fori_loop(0, C, one, 0)
-def prep_lhs(v_ref, a_ref, n):
-    for i in range(16):
+def prep_lhs(v_ref, a_ref, n, part=range(16)):
+    for i in part:
         x = jnp.concatenate([jnp.concatenate([v_ref.at[p][pl.ds(n*32 + 2*i + d, 8, stride=SEGR), :] for p in range(2)], axis=1) for d in range(2)], axis=0)
-        hi, lo = split(x)
+        hi, lo = split_left(x)
         a_ref[16*i:16*i+16, 0:256] = hi
-        a_ref[16*i:16*i+16, 256:512] = hi
-        a_ref[16*i:16*i+16, 512:768] = lo
-def mm(a_ref, b_ref, g_ref, n):
+        a_ref[16*i:16*i+16, 256:512] = lo
+def mm(a_ref, b_ref, g_ref, n, tiles=range(9)):
     def rows(c):
         return b_ref[pl.ds(pl.multiple_of(c*BR + n*16, 16), 128), :]
-    for j in range(9):
+    for j in tiles:
         cs = [2*j, 2*j+1] if j < 8 else [16]
         b = jnp.concatenate([rows(c) for c in cs], axis=0)
         g_ref[:, cs[0]*128:(cs[-1]+1)*128] = lax.dot_general(a_ref[...], b, DT, preferred_element_type=jnp.float32)
@@ -50,7 +54,7 @@
     return ((s & 15) >> 1)*16 + (s & 1)*8 + (s >> 4)
 def take(x, idx):
     return jnp.take_along_axis(x, idx, axis=1)
-def vblock(cur, prev, n, E, R, acc_ref, lo, hi):
+def vblock(cur, prev, n, E, R, acc_ref, lo, hi, beside=None):
     lane = lax.broadcasted_iota(jnp.int32, (8,128), 1)
     rel = seg_of(lane, 0)
     prv1, nxt1, nxt2 = lane_of(rel + 127), lane_of(rel + 1), lane_of(rel + 2)
@@ -59,11 +63,11 @@
     keepb = (sg >= 2) & (sg <= 122)
     keepc = (sg >= 1) & (sg <= 121)
     neg = jnp.float32(NEG)
-    acc = jnp.full((8, 128), NEG, jnp.float32)
-    spot = (n & 3)*32
     E = [take(e, nxt2) for e in E]
     R = [take(r, nxt2) for r in R]
     for k in range(32):
+        if beside is not None and k % 4 == 0:
+            beside(k // 4)
         g = lambda ref, c: ref[k*8:k*8+8, c*128:(c+1)*128]
         N = []
         for c in range(C):
@@ -77,9 +81,9 @@
             mb = functools.reduce(jnp.maximum, E[0:5])
             mc = functools.reduce(jnp.maximum, E[14:17])
             m = jnp.maximum(jnp.where(keepx, mx, neg), jnp.maximum(jnp.where(keepb, mb, neg), jnp.where(keepc, mc, neg)))
-            acc = jnp.where(lane == spot + k, jnp.max(m, axis=1, keepdims=True), acc)
-    tile = acc_ref.at[:, pl.ds(pl.multiple_of((n >> 2)*128, 128), 128)]
-    tile[...] = jnp.where((lane >> 5) == (n & 3), acc, tile[...])
+            acc_ref[pl.ds(pl.multiple_of((n*32 + k - 31)*8, 8), 8), :] = m
+    if beside is not None:
+        beside(8)
     return E, R
 def compute(v_ref, a, b_ref, gs, acc_ref, service):
     z = jnp.zeros((8,128), jnp.float32)
@@ -90,16 +94,17 @@
     for n in range(3):
         prep_lhs(v_ref, a[n], n)
     mm(a[0], b_ref, gs[0], 0)
-    mm(a[1], b_ref, gs[1], 1)
-    E, R = vblock(gs[0], gs[2], first, E, R, acc_ref, 31, 32)
+    E, R = vblock(gs[0], gs[2], first, E, R, acc_ref, 31, 32, lambda j: mm(a[1], b_ref, gs[1], 1, [j]))
     def three(m, carry):
         E, R = list(carry[0]), list(carry[1])
         service(m)
         for r in range(3):
             n = 1 + 3*m + r
-            mm(a[(2+r)%3], b_ref, gs[(2+r)%3], n+1)
-            prep_lhs(v_ref, a[r%3], jnp.minimum(n+2, NB-1))
-            E, R = vblock(gs[(1+r)%3], gs[r%3], n, E, R, acc_ref, 0, 32)
+            def beside(j, n=n, r=r):
+                mm(a[(2+r)%3], b_ref, gs[(2+r)%3], n+1, [j])
+                if j < 8:
+                    prep_lhs(v_ref, a[r%3], jnp.minimum(n+2, NB-1), [2*j, 2*j+1])
+            E, R = vblock(gs[(1+r)%3], gs[r%3], n, E, R, acc_ref, 0, 32, beside)
         return tuple(E), tuple(R)
     E, R = lax.fori_loop(0, 5, three, (tuple(E), tuple(R)))
     E, R = vblock(gs[1], gs[0], first + 16, list(E), list(R), acc_ref, 0, 31)
@@ -107,12 +112,12 @@
     back = lane_of(lane - 32)
     return [take(r, back) for r in R]
 def finish(acc_ref, R, col_ref, row_ref):
-    lane = lax.broadcasted_iota(jnp.int32, (8, 128), 1)
-    turned = [pltpu.roll(acc_ref[:, 128*j:128*(j+1)], 97, 1) for j in range(5)]
-    for j in range(4):
-        best = jnp.where(lane < 97, turned[j], turned[j+1])*(1.0/M)
-        for s in range(8):
-            col_ref[s, 0:1, 128*j:128*(j+1)] = best[s:s+1]
+    def one(s, _):
+        for tb in range(4):
+            x = acc_ref[pl.ds(s + tb*1024, 128, stride=8), :]
+            col_ref[s, 0:1, tb*128:(tb+1)*128] = jnp.max(x.T, axis=0, keepdims=True)*(1.0/M)
+        return 0
+    lax.fori_loop(0, 8, one, 0)
     rows = jnp.concatenate([jnp.max(r, axis=0, keepdims=True) for r in R] + [jnp.full((7, 128), NEG, jnp.float32)], axis=0)*(1.0/M)
     for j in range(4):
         q = lax.broadcasted_iota(jnp.int32, (128, 512), 1) + (31 + 512*j)
@@ -380,7 +385,6 @@
         pl.when(m == 2)(third)
         pl.when(m == 3)(lambda: others(3))
 
-    acc[...] = jnp.full(acc.shape, NEG, F32)
     R = compute(v_ref, [a0, a1, a2], bt, [g0, g1, g2], acc, service)
     finish(acc, R, colm, rowm)
     for c, when in waits:
@@ -427,9 +431,9 @@
         scratch_shapes=[
             pltpu.VMEM((2, 8*SEGR, 128), F32), pltpu.VMEM((2, 2176, 128), F32),
             pltpu.VMEM((2, 128, 128), F32), pltpu.VMEM((2, 2, 32, 128), F32),
-            pltpu.VMEM((256, 768), jnp.bfloat16), pltpu.VMEM((256, 768), jnp.bfloat16), pltpu.VMEM((256, 768), jnp.bfloat16), pltpu.VMEM((C*BR, 768), jnp.bfloat16),
+            pltpu.VMEM((256, 512), jnp.bfloat16), pltpu.VMEM((256, 512), jnp.bfloat16), pltpu.VMEM((256, 512), jnp.bfloat16), pltpu.VMEM((C*BR, 512), jnp.bfloat16),
             pltpu.VMEM((256, C*128), F32), pltpu.VMEM((256, C*128), F32), pltpu.VMEM((256, C*128), F32),
-            pltpu.VMEM((8, 640), F32),
+            pltpu.VMEM((4096, 128), F32),
             pltpu.VMEM((8, 1, 512), F32), pltpu.VMEM((16, 1, 128), F32),
             pltpu.VMEM((8, 1, 512), F32), pltpu.VMEM((16, 1, 128), F32),
             DMA((140,)), DMA((8, NQ)), DMA((16, 2)), DMA((3,)),

time: 66.1 us -> 62.3 us (0.943)
  Pallas kernels: 63.6 us -> 59.8 us
    pallas_call x1, Pallas kernels: 63.6 us -> 59.8 us  [on_device(): pl.pallas_call(kern, out_shape=(jax.ShapeDtypeStruct((1, 512), F32), jax....]
where the time goes in v6:
time: 62.3 us; the launch traced here: 62.2 us
  Pallas kernels  59.8 us (96%)
  local copies, waits for them, and re-layouts  1.71 us (3%)
  between operations  0.66 us (1%)
    pallas_call x1, Pallas kernels, on_device(): pl.pallas_call(kern, out_shape=(jax.ShapeDtypeStruct((1, 512), F32), jax....  59.8 us
    unnamed x6, local copies, waits for them, and re-layouts  1.71 us

profile of v6, /device:TPU:1, one launch (start us, length us, event | category | flops | bytes accessed | tf_op | source)
XLA Modules:
  0.0 62.2 jit_solution(5960938449306240101)
XLA Ops:
  0.6 59.8 %join_profile.1 = (f32[1,512]{1,0:T(1,128)}, f32[1,128]{1,0:T(1,128)}) custom-call(f32[128,256]{1,0:T(8,128)} %s_ref.1, f32[31,256]{1,0:T(8,128)} %st_ref.1, f32[512,256]{1,0:T(8,128)} %a_ref.1, f32[31,256]{1,0:T(8,128)} %at_ref.1), custom_call_target="tpu_custom_call" | custom-call | tf_op jit(solution)/shard_map/join_profile/pallas_call | solution.py:427
  60.5 0.0 copy-start.1
  60.5 0.0 copy-start
  60.5 0.6 copy-done.1
  61.1 0.5 copy.8
  61.6 0.0 copy-done
  61.6 0.6 copy.9
Async XLA Ops:
  60.5 0.6 %copy-start.1 = (f32[1,128]{1,0:T(1,128)S(1)}, f32[1,128]{1,0:T(1,128)}, u32[]{:S(2)}) copy-start(f32[1,128]{1,0:T(1,128)} %get-tuple-element.4) | copy-start | bytes 1540
  60.5 1.1 %copy-start = (f32[1,512]{1,0:T(1,128)S(1)}, f32[1,512]{1,0:T(1,128)}, u32[]{:S(2)}) copy-start(f32[1,512]{1,0:T(1,128)} %get-tuple-element.5) | copy-start | bytes 6148

commit v7 on v6

--- a/solution.py
+++ b/solution.py
@@ -111,13 +111,14 @@
     lane = lax.broadcasted_iota(jnp.int32, (8,128), 1)
     back = lane_of(lane - 32)
     return [take(r, back) for r in R]
-def finish(acc_ref, R, col_ref, row_ref):
+def finish_cols(acc_ref, col_ref):
     def one(s, _):
         for tb in range(4):
             x = acc_ref[pl.ds(s + tb*1024, 128, stride=8), :]
             col_ref[s, 0:1, tb*128:(tb+1)*128] = jnp.max(x.T, axis=0, keepdims=True)*(1.0/M)
         return 0
     lax.fori_loop(0, 8, one, 0)
+def finish_rows(R, row_ref):
     rows = jnp.concatenate([jnp.max(r, axis=0, keepdims=True) for r in R] + [jnp.full((7, 128), NEG, jnp.float32)], axis=0)*(1.0/M)
     for j in range(4):
         q = lax.broadcasted_iota(jnp.int32, (128, 512), 1) + (31 + 512*j)
@@ -386,7 +387,7 @@
         pl.when(m == 3)(lambda: others(3))
 
     R = compute(v_ref, [a0, a1, a2], bt, [g0, g1, g2], acc, service)
-    finish(acc, R, colm, rowm)
+    finish_rows(R, rowm)
     for c, when in waits:
         if when is None:
             c.wait_send()
@@ -399,20 +400,21 @@
         else:
             pl.when(how[1])(lambda index=index: arrived(us(0, 0), send.at[index]))
     cp = []
+    for j in range(16):
+        other = jnp.logical_or(col != j, away)
+        c = pltpu.make_async_remote_copy(src_ref=rowm.at[j], dst_ref=rbuf.at[me_r], send_sem=rsend.at[j], recv_sem=rgot.at[me_r], device_id=(rb, j), device_id_type=MESH)
+        pl.when(other)(c.start)
+        cp.append((c, other))
+    lr = pltpu.make_async_copy(rowm.at[col], rbuf.at[me_r], rgot.at[me_r])
+    pl.when(home)(lr.start)
+    finish_cols(acc, colm)
     for s in range(8):
         other = rb != s
         c = pltpu.make_async_remote_copy(src_ref=colm.at[s], dst_ref=cbuf.at[rb], send_sem=csend.at[s], recv_sem=cgot.at[rb], device_id=dev(x, y, s // 2, s % 2), device_id_type=MESH)
         pl.when(other)(c.start)
         cp.append((c, other))
-    for j in range(16):
-        other = jnp.logical_or(col != j, away)
-        c = pltpu.make_async_remote_copy(src_ref=rowm.at[j], dst_ref=rbuf.at[me_r], send_sem=rsend.at[j], recv_sem=rgot.at[me_r], device_id=(rb, j), device_id_type=MESH)
-        pl.when(other)(c.start)
-        cp.append((c, other))
     lc = pltpu.make_async_copy(colm.at[rb], cbuf.at[rb], cgot.at[rb])
-    lr = pltpu.make_async_copy(rowm.at[col], rbuf.at[me_r], rgot.at[me_r])
     lc.start()
-    pl.when(home)(lr.start)
     for s in range(8):
         arrived(cbuf.at[s], cgot.at[s])
     for j in range(16):

time: 62.3 us -> 61.1 us (0.981)
  Pallas kernels: 59.8 us -> 58.5 us
    pallas_call x1, Pallas kernels: 59.8 us -> 58.5 us  [on_device(): pl.pallas_call(kern, out_shape=(jax.ShapeDtypeStruct((1, 512), F32), jax....]
where the time goes in v7:
time: 61.1 us; the launch traced here: 60.9 us
  Pallas kernels  58.5 us (96%)
  local copies, waits for them, and re-layouts  1.71 us (3%)
  between operations  0.66 us (1%)
    pallas_call x1, Pallas kernels, on_device(): pl.pallas_call(kern, out_shape=(jax.ShapeDtypeStruct((1, 512), F32), jax....  58.5 us
    unnamed x6, local copies, waits for them, and re-layouts  1.71 us

profile of v7, /device:TPU:1, one launch (start us, length us, event | category | flops | bytes accessed | tf_op | source)
XLA Modules:
  0.0 60.9 jit_solution(13297161766548114071)
XLA Ops:
  0.6 58.5 %join_profile.1 = (f32[1,512]{1,0:T(1,128)}, f32[1,128]{1,0:T(1,128)}) custom-call(f32[128,256]{1,0:T(8,128)} %s_ref.1, f32[31,256]{1,0:T(8,128)} %st_ref.1, f32[512,256]{1,0:T(8,128)} %a_ref.1, f32[31,256]{1,0:T(8,128)} %at_ref.1), custom_call_target="tpu_custom_call" | custom-call | tf_op jit(solution)/shard_map/join_profile/pallas_call | solution.py:429
  59.2 0.0 copy-start.1
  59.2 0.0 copy-start
  59.2 0.6 %copy-done.1 = f32[1,128]{1,0:T(1,128)S(1)} copy-done((f32[1,128]{1,0:T(1,128)S(1)}, f32[1,128]{1,0:T(1,128)}, u32[]{:S(2)}) %copy-start.1) | copy-done | bytes 536
  59.8 0.5 copy.8
  60.3 0.0 copy-done
  60.3 0.6 copy.9
Async XLA Ops:
  59.2 0.6 %copy-start.1 = (f32[1,128]{1,0:T(1,128)S(1)}, f32[1,128]{1,0:T(1,128)}, u32[]{:S(2)}) copy-start(f32[1,128]{1,0:T(1,128)} %get-tuple-element.4) | copy-start | bytes 1540
  59.2 1.1 %copy-start = (f32[1,512]{1,0:T(1,128)S(1)}, f32[1,512]{1,0:T(1,128)}, u32[]{:S(2)}) copy-start(f32[1,512]{1,0:T(1,128)} %get-tuple-element.5) | copy-start | bytes 6148
